TPU v7x, 32 devices: a whole 2x2x4 slice. The times are simulated.
32 devices in a mesh: lead: 8 (over z, x), space: 4 (over y, core).
Axes of the slice: x: 2, y: 2, z: 4, core: 2. Of those that a mesh axis runs over, the one named last changes fastest.
Arguments:
- latents: bfloat16 [8, 64, 128, 1024], P('lead', 'space'), may hold values from -6 to 6
- owners: int32 [2], replicated, may hold values from 0 to 7, as said below
- lead_ids: int32 [8], P('lead'), may hold values from 0 to 359
- film_scale: float32 [360, 1024], replicated, may hold values from -3 to 3
- film_shift: float32 [360, 1024], replicated, may hold values from -3 to 3
- w_qkv_row: bfloat16 [1024, 3072], P('space'), may hold values from -0.1875 to 0.1875
- w_out_row: bfloat16 [1024, 1024], P('space'), may hold values from -0.1875 to 0.1875
- gain_col: float32 [1024], replicated, may hold values from 0.25 to 1.75
- w_qkv_col: bfloat16 [1024, 3072], P('space'), may hold values from -0.1875 to 0.1875
- w_out_col: bfloat16 [1024, 1024], P('space'), may hold values from -0.1875 to 0.1875
Outputs:
- result: bfloat16 [8, 64, 128, 1024], P('lead', None, 'space')
Inputs may be any that keep to these rules, and one draw needn't show every extreme that they name: `owners`: the two analysis times are held by two different lead groups, one of which is the last lead group.
All inputs are finite; a program needn't handle non-finite values.
Results may differ from a plain program's by a relative error of at most 0.013.
Values may be sent and summed in bfloat16 or wider, within the bound.
No kernel may reach another device: no remote copies, remote signals or barrier semaphores. Data moves between devices by JAX's collectives and lax.ppermute only.
A program may use at most 128 MiB of HBM per device.

v0:
```python
import math

import jax
import jax.numpy as jnp
from jax import lax
from jax.experimental import pallas as pl
from jax.experimental.pallas import tpu as pltpu
from jax.sharding import PartitionSpec as P


HEADS = 8
EPS = 1e-06
NEG = -1e30
BLOCK = 128
TILE = 512
CHUNKS = 4
F32 = jnp.float32
BF16 = jnp.bfloat16


def dot(a, b):
    return jnp.dot(a, b, preferred_element_type=F32)


def dot_t(a, b):
    return lax.dot_general(a, b, (((1,), (1,)), ((), ())), preferred_element_type=F32)


def fetch(pieces, space, w_ref, sems):
    channels = w_ref.shape[0]
    pair = 2 * channels // HEADS
    groups = [[], [], []]
    for j, (w_qkv, w_out) in enumerate(pieces):
        deep = w_out.shape[0]
        at = pl.ds(pl.multiple_of((space ^ j) * deep, deep), deep)
        for c in range(3):
            for g, low, high in ((0, 0, pair), (1, pair, channels)):
                lane = slice(c * channels + low, c * channels + high)
                groups[g].append(
                    pltpu.make_async_copy(
                        w_qkv.at[:, lane], w_ref.at[at, lane], sems.at[2 * c + g, j]
                    )
                )
        groups[2].append(
            pltpu.make_async_copy(w_out, w_ref.at[at, 3 * channels :], sems.at[6, j])
        )
    return groups


def paired(refs):
    return list(zip(refs[::2], refs[1::2]))


def weight_scratch(channels, n_space):
    return [
        pltpu.VMEM((channels, 4 * channels), BF16),
        pltpu.SemaphoreType.DMA((7, n_space)),
    ]


class Pairs:
    def __init__(self, tokens, channels, keep):
        self.head = channels // HEADS
        self.pair = 2 * self.head
        self.factor = math.log2(math.e) / math.sqrt(self.head)
        self.keep = keep
        self.units = [
            (slice(b * BLOCK, (b + 1) * BLOCK), j * self.head)
            for b in range(tokens // BLOCK)
            for j in range(2)
        ]

    def scores(self, qkv):
        q, k, _ = qkv
        return [
            dot_t(q[r, c : c + self.head], k[r, c : c + self.head]) for r, c in self.units
        ]

    def mix(self, scores, qkv, mix_ref, lane):
        v = qkv[2]
        ones = jnp.ones((BLOCK, self.head), BF16)
        weights = []
        for s in scores:
            if self.keep is not None:
                s = jnp.where(self.keep, s, NEG)
            top = jnp.max(s, axis=-1, keepdims=True)
            weights.append(jnp.exp2((s - top) * self.factor).astype(BF16))
        for e, (r, c) in zip(weights, self.units):
            both = dot(e, jnp.concatenate([v[r, c : c + self.head], ones], axis=1))
            mix_ref[r, lane + c : lane + c + self.head] = (
                both[:, : self.head] / both[:, self.head :]
            ).astype(BF16)

    def project(self, x, w_ref, p):
        channels = w_ref.shape[0]
        first = p * self.pair
        return [
            dot(x, w_ref[:, c * channels + first : c * channels + first + self.pair]).astype(BF16)
            for c in range(3)
        ]


def row_kernel(n_space, place_ref, *refs):
    mine_ref, other_ref, gain_ref, bias_ref = refs[:4]
    pieces = paired(refs[4 : 4 + 2 * n_space])
    outs = refs[4 + 2 * n_space : 4 + 3 * n_space]
    h_ref, mix_ref, y_ref, w_ref, sems = refs[4 + 3 * n_space :]
    half, width, channels = mine_ref.shape
    part = width // n_space
    space = place_ref[0]
    side = place_ref[1]
    groups = fetch(pieces, space, w_ref, sems)
    for group in groups:
        for copy in group:
            copy.start()
    tokens = half * width
    for n, ref in enumerate((mine_ref, other_ref)):
        x = ref[...].reshape(tokens, channels).astype(F32)
        inverse = lax.rsqrt(jnp.mean(x * x, axis=-1, keepdims=True) + EPS)
        h_ref[n * tokens : (n + 1) * tokens, :] = (
            x * inverse * gain_ref[...] + bias_ref[...]
        ).astype(BF16)
    pairs = Pairs(2 * tokens, channels, None)
    for copy in groups[0]:
        copy.wait()
    ahead = pairs.project(h_ref[...], w_ref, 0)
    for p in range(HEADS // 2):
        qkv = ahead
        scores = pairs.scores(qkv)
        if p < 2:
            for copy in groups[p + 1]:
                copy.wait()
        if p + 1 < HEADS // 2:
            ahead = pairs.project(h_ref[...], w_ref, p + 1)
        pairs.mix(scores, qkv, mix_ref, p * pairs.pair)
    y = dot(mix_ref[...], w_ref[:, 3 * channels :])
    y = (y + h_ref[...].astype(F32)).astype(BF16)
    for n in range(2):
        at = pl.ds((side ^ n) * half, half)
        y_ref[at] = y[n * tokens : (n + 1) * tokens].reshape(half, width, channels)
    for j, out in enumerate(outs):
        at = pl.ds(pl.multiple_of((space ^ j) * part, part), part)
        out[...] = y_ref[:, at, :]


def row_call(place, mine, other, gain, bias, pieces):
    half, width, channels = mine.shape
    n_space = len(pieces)
    part = width // n_space
    tokens = 2 * half * width
    vmem = pl.BlockSpec(memory_space=pltpu.VMEM)
    return pl.pallas_call(
        lambda *refs: row_kernel(n_space, *refs),
        out_shape=[jax.ShapeDtypeStruct((2 * half, part, channels), BF16)] * n_space,
        in_specs=[pl.BlockSpec(memory_space=pltpu.SMEM)]
        + [vmem] * 4
        + [pl.BlockSpec(memory_space=pl.ANY)] * (2 * n_space),
        out_specs=[vmem] * n_space,
        scratch_shapes=[
            pltpu.VMEM((tokens, channels), BF16),
            pltpu.VMEM((tokens, channels), BF16),
            pltpu.VMEM((2 * half, width, channels), BF16),
            *weight_scratch(channels, n_space),
        ],
        compiler_params=pltpu.CompilerParams(vmem_limit_bytes=60 << 20),
        cost_estimate=pl.CostEstimate(
            flops=tokens * channels * (8 * channels + 4 * width),
            bytes_accessed=4 * tokens * channels + 8 * channels * channels,
            transcendentals=0,
        ),
        name="row_attention",
    )(place, mine, other, gain, bias, *[w for piece in pieces for w in piece])


def col_kernel(n_chunks, n_space, place_ref, *refs):
    count = n_chunks * n_space
    chunks = refs[:count]
    gain_ref = refs[count]
    pieces = paired(refs[count + 1 : count + 1 + 2 * n_space])
    o_ref, x_ref, n_ref, mix_ref, perm_ref, w_ref, sems = refs[count + 1 + 2 * n_space :]
    rows, cols, channels = o_ref.shape
    deep = chunks[0].shape[0]
    space = place_ref[0]
    groups = fetch(pieces, space, w_ref, sems)
    for group in groups:
        for copy in group:
            copy.start()
    for i in range(n_chunks):
        for j in range(n_space):
            first = ((space ^ j) * n_chunks + i) * deep
            x_ref[pl.ds(first, deep)] = chunks[i * n_space + j][...].astype(F32)
    keep = None
    if rows < BLOCK:
        left = lax.broadcasted_iota(jnp.int32, (BLOCK, BLOCK), 0) // rows
        keep = left == lax.broadcasted_iota(jnp.int32, (BLOCK, BLOCK), 1) // rows
    tokens = mix_ref.shape[0]
    each = tokens // rows
    tiles = cols // each
    pairs = Pairs(tokens, channels, keep)

    here = lax.broadcasted_iota(jnp.int32, (tokens, tokens), 0)
    there = lax.broadcasted_iota(jnp.int32, (tokens, tokens), 1)
    perm_ref[0] = ((here % rows) * each + here // rows == there).astype(BF16)
    perm_ref[1] = ((there % rows) * each + there // rows == here).astype(BF16)

    def wide(t):
        return x_ref[:, t * each : (t + 1) * each, :].reshape(tokens, channels)

    def prepare(t):
        x = wide(t)
        inverse = lax.rsqrt(jnp.mean(x * x, axis=-1, keepdims=True) + EPS)
        normed = (x * inverse * gain_ref[...]).astype(BF16)
        n_ref[t % 2] = dot(perm_ref[0], normed).astype(BF16)

    def finish(t):
        mixed = dot(perm_ref[1], mix_ref[...]).astype(BF16)
        y = wide(t) + dot(mixed, w_ref[:, 3 * channels :])
        x_ref[:, t * each : (t + 1) * each, :] = y.reshape(rows, each, channels)
        if (t + 1) * each % 16 == 0 or t + 1 == tiles:
            at = slice((t + 1) * each - min(16, (t + 1) * each), (t + 1) * each)
            o_ref[:, at, :] = x_ref[:, at, :].astype(BF16)

    prepare(0)
    for copy in groups[0]:
        copy.wait()
    ahead = pairs.project(n_ref[0], w_ref, 0)
    for group in groups[1:]:
        for copy in group:
            copy.wait()
    steps = [(t, p) for t in range(tiles) for p in range(HEADS // 2)]
    for n, (t, p) in enumerate(steps):
        qkv = ahead
        scores = pairs.scores(qkv)
        if n + 1 < len(steps):
            after = steps[n + 1]
            ahead = pairs.project(n_ref[after[0] % 2], w_ref, after[1])
        if p == 1 and t + 1 < tiles:
            prepare(t + 1)
        pairs.mix(scores, qkv, mix_ref, p * pairs.pair)
        if p + 1 == HEADS // 2:
            finish(t)


def col_call(place, chunks, gain, pieces):
    deep, cols, channels = chunks[0][0].shape
    n_chunks = len(chunks)
    n_space = len(pieces)
    rows = n_space * deep * n_chunks
    tokens = min(TILE, rows * cols)
    vmem = pl.BlockSpec(memory_space=pltpu.VMEM)
    return pl.pallas_call(
        lambda *refs: col_kernel(n_chunks, n_space, *refs),
        out_shape=jax.ShapeDtypeStruct((rows, cols, channels), BF16),
        in_specs=[pl.BlockSpec(memory_space=pltpu.SMEM)]
        + [vmem] * (n_chunks * n_space + 1)
        + [pl.BlockSpec(memory_space=pl.ANY)] * (2 * n_space),
        out_specs=vmem,
        scratch_shapes=[
            pltpu.VMEM((rows, cols, channels), F32),
            pltpu.VMEM((2, tokens, channels), BF16),
            pltpu.VMEM((tokens, channels), BF16),
            pltpu.VMEM((2, tokens, tokens), BF16),
            *weight_scratch(channels, n_space),
        ],
        compiler_params=pltpu.CompilerParams(vmem_limit_bytes=60 << 20),
        cost_estimate=pl.CostEstimate(
            flops=rows * cols * channels * (8 * channels + 4 * rows),
            bytes_accessed=4 * rows * cols * channels + 8 * channels * channels,
            transcendentals=0,
        ),
        name="col_attention",
    )(
        place,
        *[piece for chunk in chunks for piece in chunk],
        gain,
        *[w for piece in pieces for w in piece],
    )


def on_device(
    latents,
    owners,
    lead_ids,
    film_scale,
    film_shift,
    w_qkv_row,
    w_out_row,
    gain_col,
    w_qkv_col,
    w_out_col,
):
    slab = latents[0]
    rows, _, _ = slab.shape
    n_lead = lax.axis_size("lead")
    n_space = lax.axis_size("space")
    lead = lax.axis_index("lead")
    space = lax.axis_index("space")
    side = lead % 2
    depth = n_lead // 2
    chunks = chunk_count(rows)
    half = rows // (2 * chunks)
    place = jnp.stack([space, side]).astype(jnp.int32)
    owned = jnp.sum((owners == lead).astype(BF16))

    def own_half(i, which):
        return lax.dynamic_slice_in_dim(slab, (2 * i + which) * half, half, 0) * owned

    sends, keeps = lax.optimization_barrier(
        ([own_half(i, 1 - side) for i in range(chunks)], [own_half(i, side) for i in range(chunks)])
    )
    swap = [(l, l ^ 1) for l in range(n_lead)]
    hops = [
        [
            pair
            for s in range(2)
            for pair in (
                ((depth - h) * 2 + s, (depth - h - 1) * 2 + s),
                ((h - 1) * 2 + s, h * 2 + s),
            )
        ]
        for h in range(1, depth)
    ]

    def across(value, j):
        return lax.ppermute(value, "space", [(s, s ^ j) for s in range(n_space)])

    bits = [1 << b for b in reversed(range(n_space.bit_length() - 1))]

    def spread(held, bit):
        return {**held, **{j ^ bit: [across(w, bit) for w in v] for j, v in held.items()}}

    film_gain = 1.0 + lax.dynamic_slice_in_dim(film_scale, lead_ids[0], 1, 0)
    film_bias = lax.dynamic_slice_in_dim(film_shift, lead_ids[0], 1, 0)
    row_held = {0: [w_qkv_row, w_out_row]}
    col_held = {0: [w_qkv_col, w_out_col]}

    row_held = spread(row_held, bits[0])
    col_held = spread(col_held, bits[0])
    for bit in bits[1:]:
        row_held = spread(row_held, bit)
        col_held = spread(col_held, bit)
    row_pieces = [row_held[j] for j in range(n_space)]

    exchanged = []
    for i in range(chunks):
        got = lax.ppermute(sends[i], "lead", swap)
        own = keeps[i] + got
        terms = [own]
        for h, pairs in enumerate(hops):
            send = own if h == 0 else own + terms[-1]
            terms.append(lax.ppermute(send, "lead", pairs))
        mine = terms[0]
        for got in terms[1:]:
            mine = mine + got
        other = lax.ppermute(mine, "lead", swap)
        outs = row_call(place, mine, other, film_gain, film_bias, row_pieces)
        exchanged.append([outs[0]] + [across(outs[j], j) for j in range(1, n_space)])

    result = col_call(
        place,
        exchanged,
        gain_col[None, :],
        [col_held[j] for j in range(n_space)],
    )
    return result[None]


def chunk_count(rows):
    return min(CHUNKS, rows // 2)


def solution(mesh):
    placed = (
        P("lead", "space", None, None),
        P(),
        P("lead"),
        P(),
        P(),
        P("space", None),
        P("space", None),
        P(),
        P("space", None),
        P("space", None),
    )

    return jax.shard_map(
        on_device,
        mesh=mesh,
        in_specs=placed,
        out_specs=P("lead", None, "space", None),
        check_vma=False,
    )
```

profile of v0, /device:TPU:0, one launch (start us, length us, event | category | flops | bytes accessed | tf_op | source)
XLA Modules:
  0.0 260.7 jit_solution(403071032815303535)
XLA Ops:
  0.0 1.3 fusion
  1.3 3.2 %multiply_bitcast_fusion = (bf16[2,128,1024]{2,1,0:T(8,128)(2,1)S(1)}, bf16[2,128,1024]{2,1,0:T(8,128)(2,1)S(1)}, bf16[2,128,1024]{2,1,0:T(8,128)(2,1)S(1)}, bf1...) fusion(bf16[1,16,128,1024]{3,2,1,0:T(8,128)(2,1)} %param.10, ...), kind=kLoop, calls=%fused_computation.4 | loop fusion | flops 2097152 | bytes 8388642 | tf_op jit(solution)/shard_map/mul | solution.py:306
  4.5 3.0 %collective-permute-start.30 = (bf16[2,128,1024]{2,1,0:T(8,128)(2,1)S(1)}, bf16[2,128,1024]{2,1,0:T(8,128)(2,1)S(1)}, u32[]{:S(2)}, u32[]{:S(2)}) collective-permute-start(bf16[2,128,1024]{2,1,0:T(8,128)(2,1)S(1)} %get-tuple-element.48), channel_id=1, source_target_pairs={{0,4},{4,0},{8,12},{12,8},{16,20},{20,16},{24,28},{28,24},{1,5},{5... | collective-permute-start | bytes 1572872 | tf_op jit(solution)/shard_map/ppermute | solution.py:346
  7.5 1.5 collective-permute-start.8
  9.6 1.5 collective-permute-start.14
  11.1 9.2 %collective-permute-done.30 = bf16[2,128,1024]{2,1,0:T(8,128)(2,1)S(1)} collective-permute-done((bf16[2,128,1024]{2,1,0:T(8,128)(2,1)S(1)}, bf16[2,128,1024]{2,1,0:T(8,128)(2,1)S(1)}, u32[]{:S(2)}, u32[]{:S(2)}) %collective-permute-start.30) | collective-permute-done | bytes 524320 | tf_op jit(solution)/shard_map/ppermute | solution.py:346
  20.3 2.0 collective-permute-start
  22.3 1.6 collective-permute-start.41
  24.1 7.4 %collective-permute-done.22 = bf16[2,128,1024]{2,1,0:T(8,128)(2,1)S(1)} collective-permute-done((bf16[2,128,1024]{2,1,0:T(8,128)(2,1)S(1)}, bf16[2,128,1024]{2,1,0:T(8,128)(2,1)S(1)}, u32[]{:S(2)}, u32[]{:S(2)}) %collective-permute-start.22) | collective-permute-done | bytes 524320 | tf_op jit(solution)/shard_map/ppermute | solution.py:346
  31.5 4.0 %collective-permute-start.31 = (bf16[2,128,1024]{2,1,0:T(8,128)(2,1)S(1)}, bf16[2,128,1024]{2,1,0:T(8,128)(2,1)S(1)}, u32[]{:S(2)}, u32[]{:S(2)}) collective-permute-start(bf16[2,128,1024]{2,1,0:T(8,128)(2,1)S(1)} %add.156), channel_id=1, source_target_pairs={{24,16},{0,8},{28,20},{4,12},{25,17},{1,9},{29,21},{5,13},{26,18},... | collective-permute-start | bytes 1572872 | tf_op jit(solution)/shard_map/ppermute | solution.py:351
  35.9 6.9 %collective-permute-done.14 = bf16[2,128,1024]{2,1,0:T(8,128)(2,1)S(1)} collective-permute-done((bf16[2,128,1024]{2,1,0:T(8,128)(2,1)S(1)}, bf16[2,128,1024]{2,1,0:T(8,128)(2,1)S(1)}, u32[]{:S(2)}, u32[]{:S(2)}) %collective-permute-start.14) | collective-permute-done | bytes 524320 | tf_op jit(solution)/shard_map/ppermute | solution.py:346
  42.8 4.0 %collective-permute-start.23 = (bf16[2,128,1024]{2,1,0:T(8,128)(2,1)S(1)}, bf16[2,128,1024]{2,1,0:T(8,128)(2,1)S(1)}, u32[]{:S(2)}, u32[]{:S(2)}) collective-permute-start(bf16[2,128,1024]{2,1,0:T(8,128)(2,1)S(1)} %add.151), channel_id=1, source_target_pairs={{24,16},{0,8},{28,20},{4,12},{25,17},{1,9},{29,21},{5,13},{26,18},... | collective-permute-start | bytes 1572872 | tf_op jit(solution)/shard_map/ppermute | solution.py:351
  46.8 6.3 %collective-permute-done = bf16[2,128,1024]{2,1,0:T(8,128)(2,1)S(1)} collective-permute-done((bf16[2,128,1024]{2,1,0:T(8,128)(2,1)S(1)}, bf16[2,128,1024]{2,1,0:T(8,128)(2,1)S(1)}, u32[]{:S(2)}, u32[]{:S(2)}) %collective-permute-start) | collective-permute-done | bytes 524320 | tf_op jit(solution)/shard_map/ppermute | solution.py:346
  53.1 1.8 collective-permute-start.7
  55.1 3.5 %collective-permute-start.15 = (bf16[2,128,1024]{2,1,0:T(8,128)(2,1)S(1)}, bf16[2,128,1024]{2,1,0:T(8,128)(2,1)S(1)}, u32[]{:S(2)}, u32[]{:S(2)}) collective-permute-start(bf16[2,128,1024]{2,1,0:T(8,128)(2,1)S(1)} %add.146), channel_id=1, source_target_pairs={{24,16},{0,8},{28,20},{4,12},{25,17},{1,9},{29,21},{5,13},{26,18},... | collective-permute-start | bytes 1572872 | tf_op jit(solution)/shard_map/ppermute | solution.py:351
  59.2 1.3 collective-permute-start.1
  60.5 0.7 collective-permute-start.32
  61.4 9.5 %collective-permute-done.15 = bf16[2,128,1024]{2,1,0:T(8,128)(2,1)S(1)} collective-permute-done((bf16[2,128,1024]{2,1,0:T(8,128)(2,1)S(1)}, bf16[2,128,1024]{2,1,0:T(8,128)(2,1)S(1)}, u32[]{:S(2)}, u32[]{:S(2)}) %collective-permute-start.15) | collective-permute-done | bytes 524320 | tf_op jit(solution)/shard_map/ppermute | solution.py:351
  70.9 0.7 collective-permute-start.24
  71.8 0.7 collective-permute-start.16
  72.5 7.4 %collective-permute-done.1 = bf16[2,128,1024]{2,1,0:T(8,128)(2,1)S(1)} collective-permute-done((bf16[2,128,1024]{2,1,0:T(8,128)(2,1)S(1)}, bf16[2,128,1024]{2,1,0:T(8,128)(2,1)S(1)}, u32[]{:S(2)}, u32[]{:S(2)}) %collective-permute-start.1) | collective-permute-done | bytes 524320 | tf_op jit(solution)/shard_map/ppermute | solution.py:351
  80.7 0.7 collective-permute-start.2
  81.4 1.0 add.159
  82.4 1.3 collective-permute-start.33
  83.7 7.0 %collective-permute-done.7.refs_9_ = bf16[256,3072]{1,0:T(8,128)(2,1)} collective-permute-done((bf16[256,3072]{1,0:T(8,128)(2,1)}, bf16[256,3072]{1,0:T(8,128)(2,1)}, u32[]{:S(2)}, u32[]{:S(2)}) %collective-permute-start.7) | collective-permute-done | bytes 1572896 | tf_op jit(solution)/shard_map/ppermute | solution.py:325
  90.7 1.0 add.154
  91.8 0.8 copy-done.2
  92.6 1.3 collective-permute-start.25
  94.5 0.6 pad_add_fusion.refs_0_
  95.1 1.4 dynamic-slice_add_fusion
  96.9 13.1 %collective-permute-done.33 = bf16[2,128,1024]{2,1,0:T(8,128)(2,1)} collective-permute-done((bf16[2,128,1024]{2,1,0:T(8,128)(2,1)}, bf16[2,128,1024]{2,1,0:T(8,128)(2,1)}, u32[]{:S(2)}, u32[]{:S(2)}) %collective-permute-start.33) | collective-permute-done | bytes 524320 | tf_op jit(solution)/shard_map/ppermute | solution.py:351
  110.0 1.3 collective-permute-start.17
  111.3 1.1 add_add_fusion.refs_1_
  112.5 12.4 %collective-permute-done.25 = bf16[2,128,1024]{2,1,0:T(8,128)(2,1)} collective-permute-done((bf16[2,128,1024]{2,1,0:T(8,128)(2,1)}, bf16[2,128,1024]{2,1,0:T(8,128)(2,1)}, u32[]{:S(2)}, u32[]{:S(2)}) %collective-permute-start.25) | collective-permute-done | bytes 524320 | tf_op jit(solution)/shard_map/ppermute | solution.py:351
  124.9 1.5 collective-permute-start.3
  126.4 1.1 add_add_fusion.1.refs_1_
  128.1 7.9 %collective-permute-done.17 = bf16[2,128,1024]{2,1,0:T(8,128)(2,1)S(1)} collective-permute-done((bf16[2,128,1024]{2,1,0:T(8,128)(2,1)S(1)}, bf16[2,128,1024]{2,1,0:T(8,128)(2,1)S(1)}, u32[]{:S(2)}, u32[]{:S(2)}) %collective-permute-start.17) | collective-permute-done | bytes 524320 | tf_op jit(solution)/shard_map/ppermute | solution.py:351
  136.0 1.5 collective-permute-start.34
  137.6 6.4 %collective-permute-done.3 = bf16[2,128,1024]{2,1,0:T(8,128)(2,1)S(1)} collective-permute-done((bf16[2,128,1024]{2,1,0:T(8,128)(2,1)S(1)}, bf16[2,128,1024]{2,1,0:T(8,128)(2,1)S(1)}, u32[]{:S(2)}, u32[]{:S(2)}) %collective-permute-start.3) | collective-permute-done | bytes 524320 | tf_op jit(solution)/shard_map/ppermute | solution.py:351
  144.0 1.5 collective-permute-start.26
  145.6 1.3 collective-permute-done.34.refs_2_
  147.0 0.8 copy-done.22
  147.8 1.5 collective-permute-start.18
  149.3 10.5 %row_attention.7 = (bf16[4,32,1024]{2,1,0:T(8,128)(2,1)}, bf16[4,32,1024]{2,1,0:T(8,128)(2,1)}, bf16[4,32,1024]{2,1,0:T(8,128)(2,1)}, bf16[4,32,1024]{2,1,0:T(8,128)(2,1)}) custom-call(s32[2]{0:T(128)} %pad_add_fusion.refs_0_, bf16[2,128,1024]{2,1,0:T(8,128)(2,1)} %copy-done.10, bf16[2,128,1024]{2,1,0:T(8,128)(2,1)} %copy-done.22, ...), custom_call_target="tpu_custom_call" | custom-call | flops 4563402752 | bytes 10485760 | tf_op jit(solution)/shard_map/row_attention/pallas_call | solution.py:152
  159.8 0.6 collective-permute-start.4
  160.4 10.8 %row_attention.6 = (bf16[4,32,1024]{2,1,0:T(8,128)(2,1)}, bf16[4,32,1024]{2,1,0:T(8,128)(2,1)}, bf16[4,32,1024]{2,1,0:T(8,128)(2,1)}, bf16[4,32,1024]{2,1,0:T(8,128)(2,1)}) custom-call(s32[2]{0:T(128)} %pad_add_fusion.refs_0_, bf16[2,128,1024]{2,1,0:T(8,128)(2,1)} %copy-done.9, bf16[2,128,1024]{2,1,0:T(8,128)(2,1)} %collective-permute-done.26.refs_2_, ...), custom_call_target="tpu_custom_call" | custom-call | flops 4563402752 | bytes 10485760 | tf_op jit(solution)/shard_map/row_attention/pallas_call | solution.py:152
  172.2 10.5 %row_attention.5 = (bf16[4,32,1024]{2,1,0:T(8,128)(2,1)}, bf16[4,32,1024]{2,1,0:T(8,128)(2,1)}, bf16[4,32,1024]{2,1,0:T(8,128)(2,1)}, bf16[4,32,1024]{2,1,0:T(8,128)(2,1)}) custom-call(s32[2]{0:T(128)} %pad_add_fusion.refs_0_, bf16[2,128,1024]{2,1,0:T(8,128)(2,1)} %copy-done.11, bf16[2,128,1024]{2,1,0:T(8,128)(2,1)} %copy-done.21, ...), custom_call_target="tpu_custom_call" | custom-call | flops 4563402752 | bytes 10485760 | tf_op jit(solution)/shard_map/row_attention/pallas_call | solution.py:152
  182.8 1.1 collective-permute-start.37
  184.3 0.8 collective-permute-start.28
  185.1 0.8 collective-permute-start.29
  186.0 0.7 collective-permute-start.19
  186.6 10.9 %row_attention.4 = (bf16[4,32,1024]{2,1,0:T(8,128)(2,1)}, bf16[4,32,1024]{2,1,0:T(8,128)(2,1)}, bf16[4,32,1024]{2,1,0:T(8,128)(2,1)}, bf16[4,32,1024]{2,1,0:T(8,128)(2,1)}) custom-call(s32[2]{0:T(128)} %pad_add_fusion.refs_0_, bf16[2,128,1024]{2,1,0:T(8,128)(2,1)} %copy-done.8, bf16[2,128,1024]{2,1,0:T(8,128)(2,1)} %copy-done.20, ...), custom_call_target="tpu_custom_call" | custom-call | flops 4563402752 | bytes 10485760 | tf_op jit(solution)/shard_map/row_attention/pallas_call | solution.py:152
  197.6 0.8 collective-permute-start.20
  198.4 0.8 collective-permute-start.21
  199.3 0.6 collective-permute-start.11
  199.9 2.2 collective-permute-done.29.refs_12_
  202.1 1.5 collective-permute-start.12
  203.6 0.9 collective-permute-start.13
  204.5 4.4 %collective-permute-done.20.refs_7_ = bf16[4,32,1024]{2,1,0:T(8,128)(2,1)S(1)} collective-permute-done((bf16[4,32,1024]{2,1,0:T(8,128)(2,1)S(1)}, bf16[4,32,1024]{2,1,0:T(8,128)(2,1)S(1)}, u32[]{:S(2)}, u32[]{:S(2)}) %collective-permute-start.20) | collective-permute-done | bytes 262176 | tf_op jit(solution)/shard_map/ppermute | solution.py:325
  208.9 4.4 %collective-permute-done.21.refs_8_ = bf16[4,32,1024]{2,1,0:T(8,128)(2,1)S(1)} collective-permute-done((bf16[4,32,1024]{2,1,0:T(8,128)(2,1)S(1)}, bf16[4,32,1024]{2,1,0:T(8,128)(2,1)S(1)}, u32[]{:S(2)}, u32[]{:S(2)}) %collective-permute-start.21) | collective-permute-done | bytes 262176 | tf_op jit(solution)/shard_map/ppermute | solution.py:325
  213.4 6.8 %collective-permute-done.12.refs_3_ = bf16[4,32,1024]{2,1,0:T(8,128)(2,1)S(1)} collective-permute-done((bf16[4,32,1024]{2,1,0:T(8,128)(2,1)}, bf16[4,32,1024]{2,1,0:T(8,128)(2,1)S(1)}, u32[]{:S(2)}, u32[]{:S(2)}) %collective-permute-start.12) | collective-permute-done | bytes 262176 | tf_op jit(solution)/shard_map/ppermute | solution.py:325
  220.2 4.4 %collective-permute-done.13.refs_4_ = bf16[4,32,1024]{2,1,0:T(8,128)(2,1)S(1)} collective-permute-done((bf16[4,32,1024]{2,1,0:T(8,128)(2,1)}, bf16[4,32,1024]{2,1,0:T(8,128)(2,1)S(1)}, u32[]{:S(2)}, u32[]{:S(2)}) %collective-permute-start.13) | collective-permute-done | bytes 262176 | tf_op jit(solution)/shard_map/ppermute | solution.py:325
  224.7 0.6 copy-done.40
  225.3 35.1 %col_attention.1 = bf16[64,32,1024]{2,1,0:T(8,128)(2,1)} custom-call(s32[2]{0:T(128)} %pad_add_fusion.refs_0_, bf16[4,32,1024]{2,1,0:T(8,128)(2,1)} %get-tuple-element.31.refs_1_, bf16[4,32,1024]{2,1,0:T(8,128)(2,1)} %copy-done.38, bf16[4,32,1024]{2,1,0:T(8,128)(2,1)} %copy-done.39, bf16[4,32,1024]{2,1,0:T(8,128)(2,1)} %copy-done.40, ...), custom_call_target="tpu_custom_call" | custom-call | flops 17716740096 | bytes 16777216 | tf_op jit(solution)/shard_map/col_attention/pallas_call | solution.py:251
  (131 shorter events, 5.4 us)
Async XLA Ops:
  1.3 21.0 %copy-start.13 = (bf16[256,1024]{1,0:T(8,128)(2,1)S(1)}, bf16[256,1024]{1,0:T(8,128)(2,1)}, u32[]{:S(2)}) copy-start(bf16[256,1024]{1,0:T(8,128)(2,1)} %refs_19_.1) | copy-start | bytes 1572868
  4.5 15.8 %collective-permute-start.30 = (bf16[2,128,1024]{2,1,0:T(8,128)(2,1)S(1)}, bf16[2,128,1024]{2,1,0:T(8,128)(2,1)S(1)}, u32[]{:S(2)}, u32[]{:S(2)}) collective-permute-start(bf16[2,128,1024]{2,1,0:T(8,128)(2,1)S(1)} %get-tuple-element.48), channel_id=1, source_target_pairs={{0,4},{4,0},{8,12},{12,8},{16,20},{20,16},{24,28},{28,24},{1,5},{5... | collective-permute-start | bytes 1572872 | tf_op jit(solution)/shard_map/ppermute | solution.py:346
  7.5 14.8 %collective-permute-start.8 = (bf16[256,1024]{1,0:T(8,128)(2,1)S(1)}, bf16[256,1024]{1,0:T(8,128)(2,1)S(1)}, u32[]{:S(2)}, u32[]{:S(2)}) collective-permute-start(bf16[256,1024]{1,0:T(8,128)(2,1)S(1)} %copy-done.12), channel_id=1, source_target_pairs={{0,2},{1,3},{2,0},{3,1},{4,6},{5,7},{6,4},{7,5},{8,10},{9,11},{10,... | collective-permute-start | bytes 1572872 | tf_op jit(solution)/shard_map/ppermute | solution.py:325
  9.0 22.5 %collective-permute-start.22 = (bf16[2,128,1024]{2,1,0:T(8,128)(2,1)S(1)}, bf16[2,128,1024]{2,1,0:T(8,128)(2,1)S(1)}, u32[]{:S(2)}, u32[]{:S(2)}) collective-permute-start(bf16[2,128,1024]{2,1,0:T(8,128)(2,1)S(1)} %get-tuple-element.42), channel_id=1, source_target_pairs={{0,4},{4,0},{8,12},{12,8},{16,20},{20,16},{24,28},{28,24},{1,5},{5... | collective-permute-start | bytes 1572872 | tf_op jit(solution)/shard_map/ppermute | solution.py:346
  9.6 26.2 %collective-permute-start.6 = (bf16[256,1024]{1,0:T(8,128)(2,1)S(1)}, bf16[256,1024]{1,0:T(8,128)(2,1)S(1)}, u32[]{:S(2)}, u32[]{:S(2)}) collective-permute-start(bf16[256,1024]{1,0:T(8,128)(2,1)S(1)} %copy-done.12), channel_id=1, source_target_pairs={{0,1},{1,0},{2,3},{3,2},{4,5},{5,4},{6,7},{7,6},{8,9},{9,8},{10,11... | collective-permute-start | bytes 1572872 | tf_op jit(solution)/shard_map/ppermute | solution.py:325
  9.6 33.2 %collective-permute-start.14 = (bf16[2,128,1024]{2,1,0:T(8,128)(2,1)S(1)}, bf16[2,128,1024]{2,1,0:T(8,128)(2,1)S(1)}, u32[]{:S(2)}, u32[]{:S(2)}) collective-permute-start(bf16[2,128,1024]{2,1,0:T(8,128)(2,1)S(1)} %get-tuple-element.36), channel_id=1, source_target_pairs={{0,4},{4,0},{8,12},{12,8},{16,20},{20,16},{24,28},{28,24},{1,5},{5... | collective-permute-start | bytes 1572872 | tf_op jit(solution)/shard_map/ppermute | solution.py:346
  20.3 32.9 %collective-permute-start = (bf16[2,128,1024]{2,1,0:T(8,128)(2,1)S(1)}, bf16[2,128,1024]{2,1,0:T(8,128)(2,1)S(1)}, u32[]{:S(2)}, u32[]{:S(2)}) collective-permute-start(bf16[2,128,1024]{2,1,0:T(8,128)(2,1)S(1)} %get-tuple-element.30), channel_id=1, source_target_pairs={{0,4},{4,0},{8,12},{12,8},{16,20},{20,16},{24,28},{28,24},{1,5},{5... | collective-permute-start | bytes 1572872 | tf_op jit(solution)/shard_map/ppermute | solution.py:346
  22.3 36.3 %copy-start.16 = (bf16[256,1024]{1,0:T(8,128)(2,1)}, bf16[256,1024]{1,0:T(8,128)(2,1)S(1)}, u32[]{:S(2)}) copy-start(bf16[256,1024]{1,0:T(8,128)(2,1)S(1)} %collective-permute-done.8.refs_10_) | copy-start | bytes 1572868
  22.3 32.8 %collective-permute-start.41 = (bf16[256,1024]{1,0:T(8,128)(2,1)S(1)}, bf16[256,1024]{1,0:T(8,128)(2,1)S(1)}, u32[]{:S(2)}, u32[]{:S(2)}) collective-permute-start(bf16[256,1024]{1,0:T(8,128)(2,1)S(1)} %copy-done.13), channel_id=1, source_target_pairs={{0,2},{1,3},{2,0},{3,1},{4,6},{5,7},{6,4},{7,5},{8,10},{9,11},{10,... | collective-permute-start | bytes 1572872 | tf_op jit(solution)/shard_map/ppermute | solution.py:325
  31.5 27.1 %collective-permute-start.31 = (bf16[2,128,1024]{2,1,0:T(8,128)(2,1)S(1)}, bf16[2,128,1024]{2,1,0:T(8,128)(2,1)S(1)}, u32[]{:S(2)}, u32[]{:S(2)}) collective-permute-start(bf16[2,128,1024]{2,1,0:T(8,128)(2,1)S(1)} %add.156), channel_id=1, source_target_pairs={{24,16},{0,8},{28,20},{4,12},{25,17},{1,9},{29,21},{5,13},{26,18},... | collective-permute-start | bytes 1572872 | tf_op jit(solution)/shard_map/ppermute | solution.py:351
  35.8 23.2 %copy-start.17 = (bf16[256,1024]{1,0:T(8,128)(2,1)}, bf16[256,1024]{1,0:T(8,128)(2,1)S(1)}, u32[]{:S(2)}) copy-start(bf16[256,1024]{1,0:T(8,128)(2,1)S(1)} %collective-permute-done.6.refs_8_) | copy-start | bytes 1572868
  35.8 23.4 %collective-permute-start.39 = (bf16[256,1024]{1,0:T(8,128)(2,1)S(1)}, bf16[256,1024]{1,0:T(8,128)(2,1)}, u32[]{:S(2)}, u32[]{:S(2)}) collective-permute-start(bf16[256,1024]{1,0:T(8,128)(2,1)S(1)} %copy-done.13), channel_id=1, source_target_pairs={{0,1},{1,0},{2,3},{3,2},{4,5},{5,4},{6,7},{7,6},{8,9},{9,8},{10,11... | collective-permute-start | bytes 1572872 | tf_op jit(solution)/shard_map/ppermute | solution.py:325
  42.8 17.8 %collective-permute-start.23 = (bf16[2,128,1024]{2,1,0:T(8,128)(2,1)S(1)}, bf16[2,128,1024]{2,1,0:T(8,128)(2,1)S(1)}, u32[]{:S(2)}, u32[]{:S(2)}) collective-permute-start(bf16[2,128,1024]{2,1,0:T(8,128)(2,1)S(1)} %add.151), channel_id=1, source_target_pairs={{24,16},{0,8},{28,20},{4,12},{25,17},{1,9},{29,21},{5,13},{26,18},... | collective-permute-start | bytes 1572872 | tf_op jit(solution)/shard_map/ppermute | solution.py:351
  53.1 37.6 %collective-permute-start.7 = (bf16[256,3072]{1,0:T(8,128)(2,1)}, bf16[256,3072]{1,0:T(8,128)(2,1)}, u32[]{:S(2)}, u32[]{:S(2)}) collective-permute-start(bf16[256,3072]{1,0:T(8,128)(2,1)} %refs_5_.7), channel_id=1, source_target_pairs={{0,2},{1,3},{2,0},{3,1},{4,6},{5,7},{6,4},{7,5},{8,10},{9,11},{10,... | collective-permute-start | bytes 4718600 | tf_op jit(solution)/shard_map/ppermute | solution.py:325
  55.1 15.8 %collective-permute-start.15 = (bf16[2,128,1024]{2,1,0:T(8,128)(2,1)S(1)}, bf16[2,128,1024]{2,1,0:T(8,128)(2,1)S(1)}, u32[]{:S(2)}, u32[]{:S(2)}) collective-permute-start(bf16[2,128,1024]{2,1,0:T(8,128)(2,1)S(1)} %add.146), channel_id=1, source_target_pairs={{24,16},{0,8},{28,20},{4,12},{25,17},{1,9},{29,21},{5,13},{26,18},... | collective-permute-start | bytes 1572872 | tf_op jit(solution)/shard_map/ppermute | solution.py:351
  58.7 13.1 %collective-permute-start.10 = (bf16[256,1024]{1,0:T(8,128)(2,1)S(1)}, bf16[256,1024]{1,0:T(8,128)(2,1)S(1)}, u32[]{:S(2)}, u32[]{:S(2)}) collective-permute-start(bf16[256,1024]{1,0:T(8,128)(2,1)S(1)} %collective-permute-done.8.refs_10_), channel_id=1, source_target_pairs={{0,1},{1,0},{2,3},{3,2},{4,5},{5,4},{6,7},{7,6},{8,9},{9,8},{10,11... | collective-permute-start | bytes 1572872 | tf_op jit(solution)/shard_map/ppermute | solution.py:325
  59.2 20.7 %collective-permute-start.1 = (bf16[2,128,1024]{2,1,0:T(8,128)(2,1)S(1)}, bf16[2,128,1024]{2,1,0:T(8,128)(2,1)S(1)}, u32[]{:S(2)}, u32[]{:S(2)}) collective-permute-start(bf16[2,128,1024]{2,1,0:T(8,128)(2,1)S(1)} %add.138), channel_id=1, source_target_pairs={{24,16},{0,8},{28,20},{4,12},{25,17},{1,9},{29,21},{5,13},{26,18},... | collective-permute-start | bytes 1572872 | tf_op jit(solution)/shard_map/ppermute | solution.py:351
  60.5 19.4 %collective-permute-start.32 = (bf16[2,128,1024]{2,1,0:T(8,128)(2,1)S(1)}, bf16[2,128,1024]{2,1,0:T(8,128)(2,1)S(1)}, u32[]{:S(2)}, u32[]{:S(2)}) collective-permute-start(bf16[2,128,1024]{2,1,0:T(8,128)(2,1)S(1)} %add.157), channel_id=1, source_target_pairs={{16,8},{8,16},{20,12},{12,20},{17,9},{9,17},{21,13},{13,21},{18,10... | collective-permute-start | bytes 1572872 | tf_op jit(solution)/shard_map/ppermute | solution.py:351
  61.4 19.2 %copy-start = (bf16[2,128,1024]{2,1,0:T(8,128)(2,1)}, bf16[2,128,1024]{2,1,0:T(8,128)(2,1)S(1)}, u32[]{:S(2)}) copy-start(bf16[2,128,1024]{2,1,0:T(8,128)(2,1)S(1)} %add.152) | copy-start | bytes 1572868
  70.9 9.8 %collective-permute-start.24 = (bf16[2,128,1024]{2,1,0:T(8,128)(2,1)S(1)}, bf16[2,128,1024]{2,1,0:T(8,128)(2,1)S(1)}, u32[]{:S(2)}, u32[]{:S(2)}) collective-permute-start(bf16[2,128,1024]{2,1,0:T(8,128)(2,1)S(1)} %add.152), channel_id=1, source_target_pairs={{16,8},{8,16},{20,12},{12,20},{17,9},{9,17},{21,13},{13,21},{18,10... | collective-permute-start | bytes 1572872 | tf_op jit(solution)/shard_map/ppermute | solution.py:351
  71.8 10.6 %collective-permute-start.16 = (bf16[2,128,1024]{2,1,0:T(8,128)(2,1)S(1)}, bf16[2,128,1024]{2,1,0:T(8,128)(2,1)S(1)}, u32[]{:S(2)}, u32[]{:S(2)}) collective-permute-start(bf16[2,128,1024]{2,1,0:T(8,128)(2,1)S(1)} %add.147), channel_id=1, source_target_pairs={{16,8},{8,16},{20,12},{12,20},{17,9},{9,17},{21,13},{13,21},{18,10... | collective-permute-start | bytes 1572872 | tf_op jit(solution)/shard_map/ppermute | solution.py:351
  79.9 47.6 %collective-permute-start.5 = (bf16[256,3072]{1,0:T(8,128)(2,1)}, bf16[256,3072]{1,0:T(8,128)(2,1)}, u32[]{:S(2)}, u32[]{:S(2)}) collective-permute-start(bf16[256,3072]{1,0:T(8,128)(2,1)} %refs_5_.7), channel_id=1, source_target_pairs={{0,1},{1,0},{2,3},{3,2},{4,5},{5,4},{6,7},{7,6},{8,9},{9,8},{10,11... | collective-permute-start | bytes 4718600 | tf_op jit(solution)/shard_map/ppermute | solution.py:325
  79.9 47.7 %collective-permute-start.40 = (bf16[256,3072]{1,0:T(8,128)(2,1)}, bf16[256,3072]{1,0:T(8,128)(2,1)}, u32[]{:S(2)}, u32[]{:S(2)}) collective-permute-start(bf16[256,3072]{1,0:T(8,128)(2,1)} %refs_18_.1), channel_id=1, source_target_pairs={{0,2},{1,3},{2,0},{3,1},{4,6},{5,7},{6,4},{7,5},{8,10},{9,11},{10,... | collective-permute-start | bytes 4718600 | tf_op jit(solution)/shard_map/ppermute | solution.py:325
  80.7 11.1 %collective-permute-start.2 = (bf16[2,128,1024]{2,1,0:T(8,128)(2,1)S(1)}, bf16[2,128,1024]{2,1,0:T(8,128)(2,1)S(1)}, u32[]{:S(2)}, u32[]{:S(2)}) collective-permute-start(bf16[2,128,1024]{2,1,0:T(8,128)(2,1)S(1)} %add.139), channel_id=1, source_target_pairs={{16,8},{8,16},{20,12},{12,20},{17,9},{9,17},{21,13},{13,21},{18,10... | collective-permute-start | bytes 1572872 | tf_op jit(solution)/shard_map/ppermute | solution.py:351
  82.4 27.6 %collective-permute-start.33 = (bf16[2,128,1024]{2,1,0:T(8,128)(2,1)}, bf16[2,128,1024]{2,1,0:T(8,128)(2,1)}, u32[]{:S(2)}, u32[]{:S(2)}) collective-permute-start(bf16[2,128,1024]{2,1,0:T(8,128)(2,1)} %add.159), channel_id=1, source_target_pairs={{8,0},{16,24},{12,4},{20,28},{9,1},{17,25},{13,5},{21,29},{10,2},{... | collective-permute-start | bytes 1572872 | tf_op jit(solution)/shard_map/ppermute | solution.py:351
  90.7 57.0 %collective-permute-start.9 = (bf16[256,3072]{1,0:T(8,128)(2,1)}, bf16[256,3072]{1,0:T(8,128)(2,1)}, u32[]{:S(2)}, u32[]{:S(2)}) collective-permute-start(bf16[256,3072]{1,0:T(8,128)(2,1)} %collective-permute-done.7.refs_9_), channel_id=1, source_target_pairs={{0,1},{1,0},{2,3},{3,2},{4,5},{5,4},{6,7},{7,6},{8,9},{9,8},{10,11... | collective-permute-start | bytes 4718600 | tf_op jit(solution)/shard_map/ppermute | solution.py:325
  92.6 32.4 %collective-permute-start.25 = (bf16[2,128,1024]{2,1,0:T(8,128)(2,1)}, bf16[2,128,1024]{2,1,0:T(8,128)(2,1)}, u32[]{:S(2)}, u32[]{:S(2)}) collective-permute-start(bf16[2,128,1024]{2,1,0:T(8,128)(2,1)} %add.154), channel_id=1, source_target_pairs={{8,0},{16,24},{12,4},{20,28},{9,1},{17,25},{13,5},{21,29},{10,2},{... | collective-permute-start | bytes 1572872 | tf_op jit(solution)/shard_map/ppermute | solution.py:351
  96.5 14.8 %copy-start.7 = (bf16[2,128,1024]{2,1,0:T(8,128)(2,1)S(1)}, bf16[2,128,1024]{2,1,0:T(8,128)(2,1)}, u32[]{:S(2)}) copy-start(bf16[2,128,1024]{2,1,0:T(8,128)(2,1)} %copy-done.6) | copy-start | bytes 1572868
  96.7 29.7 %copy-start.1 = (bf16[2,128,1024]{2,1,0:T(8,128)(2,1)S(1)}, bf16[2,128,1024]{2,1,0:T(8,128)(2,1)}, u32[]{:S(2)}) copy-start(bf16[2,128,1024]{2,1,0:T(8,128)(2,1)} %copy-done) | copy-start | bytes 1572868
  96.7 29.7 %copy-start.5 = (bf16[2,128,1024]{2,1,0:T(8,128)(2,1)S(1)}, bf16[2,128,1024]{2,1,0:T(8,128)(2,1)}, u32[]{:S(2)}) copy-start(bf16[2,128,1024]{2,1,0:T(8,128)(2,1)} %copy-done.4) | copy-start | bytes 1572868
  110.0 26.0 %collective-permute-start.17 = (bf16[2,128,1024]{2,1,0:T(8,128)(2,1)S(1)}, bf16[2,128,1024]{2,1,0:T(8,128)(2,1)S(1)}, u32[]{:S(2)}, u32[]{:S(2)}) collective-permute-start(bf16[2,128,1024]{2,1,0:T(8,128)(2,1)S(1)} %add.149), channel_id=1, source_target_pairs={{8,0},{16,24},{12,4},{20,28},{9,1},{17,25},{13,5},{21,29},{10,2},{... | collective-permute-start | bytes 1572872 | tf_op jit(solution)/shard_map/ppermute | solution.py:351
  112.5 25.2 %copy-start.10 = (bf16[2,128,1024]{2,1,0:T(8,128)(2,1)}, bf16[2,128,1024]{2,1,0:T(8,128)(2,1)S(1)}, u32[]{:S(2)}) copy-start(bf16[2,128,1024]{2,1,0:T(8,128)(2,1)S(1)} %add_add_fusion.refs_1_) | copy-start | bytes 1572868
  124.9 19.1 %collective-permute-start.3 = (bf16[2,128,1024]{2,1,0:T(8,128)(2,1)S(1)}, bf16[2,128,1024]{2,1,0:T(8,128)(2,1)S(1)}, u32[]{:S(2)}, u32[]{:S(2)}) collective-permute-start(bf16[2,128,1024]{2,1,0:T(8,128)(2,1)S(1)} %add.141), channel_id=1, source_target_pairs={{8,0},{16,24},{12,4},{20,28},{9,1},{17,25},{13,5},{21,29},{10,2},{... | collective-permute-start | bytes 1572872 | tf_op jit(solution)/shard_map/ppermute | solution.py:351
  127.5 18.1 %copy-start.9 = (bf16[2,128,1024]{2,1,0:T(8,128)(2,1)}, bf16[2,128,1024]{2,1,0:T(8,128)(2,1)S(1)}, u32[]{:S(2)}) copy-start(bf16[2,128,1024]{2,1,0:T(8,128)(2,1)S(1)} %add_add_fusion.1.refs_1_) | copy-start | bytes 1572868
  127.5 55.3 %collective-permute-start.38 = (bf16[256,3072]{1,0:T(8,128)(2,1)}, bf16[256,3072]{1,0:T(8,128)(2,1)}, u32[]{:S(2)}, u32[]{:S(2)}) collective-permute-start(bf16[256,3072]{1,0:T(8,128)(2,1)} %refs_18_.1), channel_id=1, source_target_pairs={{0,1},{1,0},{2,3},{3,2},{4,5},{5,4},{6,7},{7,6},{8,9},{9,8},{10,11... | collective-permute-start | bytes 4718600 | tf_op jit(solution)/shard_map/ppermute | solution.py:325
  127.6 56.7 %collective-permute-start.42 = (bf16[256,3072]{1,0:T(8,128)(2,1)}, bf16[256,3072]{1,0:T(8,128)(2,1)}, u32[]{:S(2)}, u32[]{:S(2)}) collective-permute-start(bf16[256,3072]{1,0:T(8,128)(2,1)} %collective-permute-done.40.refs_22_), channel_id=1, source_target_pairs={{0,1},{1,0},{2,3},{3,2},{4,5},{5,4},{6,7},{7,6},{8,9},{9,8},{10,11... | collective-permute-start | bytes 4718600 | tf_op jit(solution)/shard_map/ppermute | solution.py:325
  136.0 10.9 %collective-permute-start.34 = (bf16[2,128,1024]{2,1,0:T(8,128)(2,1)S(1)}, bf16[2,128,1024]{2,1,0:T(8,128)(2,1)S(1)}, u32[]{:S(2)}, u32[]{:S(2)}) collective-permute-start(bf16[2,128,1024]{2,1,0:T(8,128)(2,1)S(1)} %add_add_fusion.refs_1_), channel_id=1, source_target_pairs={{0,4},{4,0},{8,12},{12,8},{16,20},{20,16},{24,28},{28,24},{1,5},{5... | collective-permute-start | bytes 1572872 | tf_op jit(solution)/shard_map/ppermute | solution.py:355
  137.6 22.2 %copy-start.11 = (bf16[2,128,1024]{2,1,0:T(8,128)(2,1)}, bf16[2,128,1024]{2,1,0:T(8,128)(2,1)S(1)}, u32[]{:S(2)}) copy-start(bf16[2,128,1024]{2,1,0:T(8,128)(2,1)S(1)} %add_add_fusion.2.refs_1_) | copy-start | bytes 1572868
  144.0 15.8 %collective-permute-start.26 = (bf16[2,128,1024]{2,1,0:T(8,128)(2,1)S(1)}, bf16[2,128,1024]{2,1,0:T(8,128)(2,1)}, u32[]{:S(2)}, u32[]{:S(2)}) collective-permute-start(bf16[2,128,1024]{2,1,0:T(8,128)(2,1)S(1)} %add_add_fusion.1.refs_1_), channel_id=1, source_target_pairs={{0,4},{4,0},{8,12},{12,8},{16,20},{20,16},{24,28},{28,24},{1,5},{5... | collective-permute-start | bytes 1572872 | tf_op jit(solution)/shard_map/ppermute | solution.py:355
  145.6 14.2 %copy-start.8 = (bf16[2,128,1024]{2,1,0:T(8,128)(2,1)}, bf16[2,128,1024]{2,1,0:T(8,128)(2,1)S(1)}, u32[]{:S(2)}) copy-start(bf16[2,128,1024]{2,1,0:T(8,128)(2,1)S(1)} %add_add_fusion.3.refs_1_) | copy-start | bytes 1572868
  147.0 24.3 %collective-permute-start.43 = (bf16[256,1024]{1,0:T(8,128)(2,1)S(1)}, bf16[256,1024]{1,0:T(8,128)(2,1)S(1)}, u32[]{:S(2)}, u32[]{:S(2)}) collective-permute-start(bf16[256,1024]{1,0:T(8,128)(2,1)S(1)} %copy-done.15), channel_id=1, source_target_pairs={{0,1},{1,0},{2,3},{3,2},{4,5},{5,4},{6,7},{7,6},{8,9},{9,8},{10,11... | collective-permute-start | bytes 1572872 | tf_op jit(solution)/shard_map/ppermute | solution.py:325
  147.8 23.6 %collective-permute-start.18 = (bf16[2,128,1024]{2,1,0:T(8,128)(2,1)S(1)}, bf16[2,128,1024]{2,1,0:T(8,128)(2,1)S(1)}, u32[]{:S(2)}, u32[]{:S(2)}) collective-permute-start(bf16[2,128,1024]{2,1,0:T(8,128)(2,1)S(1)} %add_add_fusion.2.refs_1_), channel_id=1, source_target_pairs={{0,4},{4,0},{8,12},{12,8},{16,20},{20,16},{24,28},{28,24},{1,5},{5... | collective-permute-start | bytes 1572872 | tf_op jit(solution)/shard_map/ppermute | solution.py:355
  159.8 24.1 %collective-permute-start.4 = (bf16[2,128,1024]{2,1,0:T(8,128)(2,1)S(1)}, bf16[2,128,1024]{2,1,0:T(8,128)(2,1)S(1)}, u32[]{:S(2)}, u32[]{:S(2)}) collective-permute-start(bf16[2,128,1024]{2,1,0:T(8,128)(2,1)S(1)} %add_add_fusion.3.refs_1_), channel_id=1, source_target_pairs={{0,4},{4,0},{8,12},{12,8},{16,20},{20,16},{24,28},{28,24},{1,5},{5... | collective-permute-start | bytes 1572872 | tf_op jit(solution)/shard_map/ppermute | solution.py:355
  171.3 13.8 %collective-permute-start.35 = (bf16[4,32,1024]{2,1,0:T(8,128)(2,1)}, bf16[4,32,1024]{2,1,0:T(8,128)(2,1)S(1)}, u32[]{:S(2)}, u32[]{:S(2)}) collective-permute-start(bf16[4,32,1024]{2,1,0:T(8,128)(2,1)} %get-tuple-element.50), channel_id=1, source_target_pairs={{0,1},{1,0},{2,3},{3,2},{4,5},{5,4},{6,7},{7,6},{8,9},{9,8},{10,11... | collective-permute-start | bytes 786440 | tf_op jit(solution)/shard_map/ppermute | solution.py:325
  171.4 12.6 %copy-start.35 = (bf16[4,32,1024]{2,1,0:T(8,128)(2,1)S(1)}, bf16[4,32,1024]{2,1,0:T(8,128)(2,1)}, u32[]{:S(2)}) copy-start(bf16[4,32,1024]{2,1,0:T(8,128)(2,1)} %get-tuple-element.44) | copy-start | bytes 786436
  171.4 13.0 %copy-start.33 = (bf16[4,32,1024]{2,1,0:T(8,128)(2,1)S(1)}, bf16[4,32,1024]{2,1,0:T(8,128)(2,1)}, u32[]{:S(2)}) copy-start(bf16[4,32,1024]{2,1,0:T(8,128)(2,1)} %get-tuple-element.45) | copy-start | bytes 786436
  171.4 13.7 %copy-start.29 = (bf16[4,32,1024]{2,1,0:T(8,128)(2,1)S(1)}, bf16[4,32,1024]{2,1,0:T(8,128)(2,1)}, u32[]{:S(2)}) copy-start(bf16[4,32,1024]{2,1,0:T(8,128)(2,1)} %get-tuple-element.46) | copy-start | bytes 786436
  171.4 14.5 %collective-permute-start.36 = (bf16[4,32,1024]{2,1,0:T(8,128)(2,1)}, bf16[4,32,1024]{2,1,0:T(8,128)(2,1)S(1)}, u32[]{:S(2)}, u32[]{:S(2)}) collective-permute-start(bf16[4,32,1024]{2,1,0:T(8,128)(2,1)} %get-tuple-element.51), channel_id=1, source_target_pairs={{0,2},{1,3},{2,0},{3,1},{4,6},{5,7},{6,4},{7,5},{8,10},{9,11},{10,... | collective-permute-start | bytes 786440 | tf_op jit(solution)/shard_map/ppermute | solution.py:325
  182.8 14.8 %collective-permute-start.37 = (bf16[4,32,1024]{2,1,0:T(8,128)(2,1)S(1)}, bf16[4,32,1024]{2,1,0:T(8,128)(2,1)S(1)}, u32[]{:S(2)}, u32[]{:S(2)}) collective-permute-start(bf16[4,32,1024]{2,1,0:T(8,128)(2,1)S(1)} %copy-done.34), channel_id=1, source_target_pairs={{0,3},{1,2},{2,1},{3,0},{4,7},{5,6},{6,5},{7,4},{8,11},{9,10},{10,... | collective-permute-start | bytes 786440 | tf_op jit(solution)/shard_map/ppermute | solution.py:325
  183.9 14.5 %collective-permute-start.27 = (bf16[4,32,1024]{2,1,0:T(8,128)(2,1)S(1)}, bf16[4,32,1024]{2,1,0:T(8,128)(2,1)S(1)}, u32[]{:S(2)}, u32[]{:S(2)}) collective-permute-start(bf16[4,32,1024]{2,1,0:T(8,128)(2,1)S(1)} %copy-done.35), channel_id=1, source_target_pairs={{0,1},{1,0},{2,3},{3,2},{4,5},{5,4},{6,7},{7,6},{8,9},{9,8},{10,11... | collective-permute-start | bytes 786440 | tf_op jit(solution)/shard_map/ppermute | solution.py:325
  184.3 14.9 %collective-permute-start.28 = (bf16[4,32,1024]{2,1,0:T(8,128)(2,1)S(1)}, bf16[4,32,1024]{2,1,0:T(8,128)(2,1)S(1)}, u32[]{:S(2)}, u32[]{:S(2)}) collective-permute-start(bf16[4,32,1024]{2,1,0:T(8,128)(2,1)S(1)} %copy-done.33), channel_id=1, source_target_pairs={{0,2},{1,3},{2,0},{3,1},{4,6},{5,7},{6,4},{7,5},{8,10},{9,11},{10,... | collective-permute-start | bytes 786440 | tf_op jit(solution)/shard_map/ppermute | solution.py:325
  185.1 17.0 %collective-permute-start.29 = (bf16[4,32,1024]{2,1,0:T(8,128)(2,1)S(1)}, bf16[4,32,1024]{2,1,0:T(8,128)(2,1)S(1)}, u32[]{:S(2)}, u32[]{:S(2)}) collective-permute-start(bf16[4,32,1024]{2,1,0:T(8,128)(2,1)S(1)} %copy-done.29), channel_id=1, source_target_pairs={{0,3},{1,2},{2,1},{3,0},{4,7},{5,6},{6,5},{7,4},{8,11},{9,10},{10,... | collective-permute-start | bytes 786440 | tf_op jit(solution)/shard_map/ppermute | solution.py:325
  186.0 17.7 %collective-permute-start.19 = (bf16[4,32,1024]{2,1,0:T(8,128)(2,1)}, bf16[4,32,1024]{2,1,0:T(8,128)(2,1)S(1)}, u32[]{:S(2)}, u32[]{:S(2)}) collective-permute-start(bf16[4,32,1024]{2,1,0:T(8,128)(2,1)} %get-tuple-element.38), channel_id=1, source_target_pairs={{0,1},{1,0},{2,3},{3,2},{4,5},{5,4},{6,7},{7,6},{8,9},{9,8},{10,11... | collective-permute-start | bytes 786440 | tf_op jit(solution)/shard_map/ppermute | solution.py:325
  197.6 27.0 %copy-start.25 = (bf16[4,32,1024]{2,1,0:T(8,128)(2,1)}, bf16[4,32,1024]{2,1,0:T(8,128)(2,1)S(1)}, u32[]{:S(2)}) copy-start(bf16[4,32,1024]{2,1,0:T(8,128)(2,1)S(1)} %collective-permute-done.37.refs_16_) | copy-start | bytes 786436
  197.6 11.3 %collective-permute-start.20 = (bf16[4,32,1024]{2,1,0:T(8,128)(2,1)S(1)}, bf16[4,32,1024]{2,1,0:T(8,128)(2,1)S(1)}, u32[]{:S(2)}, u32[]{:S(2)}) collective-permute-start(bf16[4,32,1024]{2,1,0:T(8,128)(2,1)S(1)} %copy-done.31), channel_id=1, source_target_pairs={{0,2},{1,3},{2,0},{3,1},{4,6},{5,7},{6,4},{7,5},{8,10},{9,11},{10,... | collective-permute-start | bytes 786440 | tf_op jit(solution)/shard_map/ppermute | solution.py:325
  198.4 26.2 %copy-start.26 = (bf16[4,32,1024]{2,1,0:T(8,128)(2,1)}, bf16[4,32,1024]{2,1,0:T(8,128)(2,1)S(1)}, u32[]{:S(2)}) copy-start(bf16[4,32,1024]{2,1,0:T(8,128)(2,1)S(1)} %collective-permute-done.27.refs_10_) | copy-start | bytes 786436
  198.4 14.9 %collective-permute-start.21 = (bf16[4,32,1024]{2,1,0:T(8,128)(2,1)S(1)}, bf16[4,32,1024]{2,1,0:T(8,128)(2,1)S(1)}, u32[]{:S(2)}, u32[]{:S(2)}) collective-permute-start(bf16[4,32,1024]{2,1,0:T(8,128)(2,1)S(1)} %copy-done.30), channel_id=1, source_target_pairs={{0,3},{1,2},{2,1},{3,0},{4,7},{5,6},{6,5},{7,4},{8,11},{9,10},{10,... | collective-permute-start | bytes 786440 | tf_op jit(solution)/shard_map/ppermute | solution.py:325
  199.3 25.3 %copy-start.27 = (bf16[4,32,1024]{2,1,0:T(8,128)(2,1)}, bf16[4,32,1024]{2,1,0:T(8,128)(2,1)S(1)}, u32[]{:S(2)}) copy-start(bf16[4,32,1024]{2,1,0:T(8,128)(2,1)S(1)} %collective-permute-done.28.refs_11_) | copy-start | bytes 786436
  199.3 14.1 %collective-permute-start.11 = (bf16[4,32,1024]{2,1,0:T(8,128)(2,1)}, bf16[4,32,1024]{2,1,0:T(8,128)(2,1)S(1)}, u32[]{:S(2)}, u32[]{:S(2)}) collective-permute-start(bf16[4,32,1024]{2,1,0:T(8,128)(2,1)} %get-tuple-element.32), channel_id=1, source_target_pairs={{0,1},{1,0},{2,3},{3,2},{4,5},{5,4},{6,7},{7,6},{8,9},{9,8},{10,11... | collective-permute-start | bytes 786440 | tf_op jit(solution)/shard_map/ppermute | solution.py:325
  202.1 22.5 %copy-start.28 = (bf16[4,32,1024]{2,1,0:T(8,128)(2,1)}, bf16[4,32,1024]{2,1,0:T(8,128)(2,1)S(1)}, u32[]{:S(2)}) copy-start(bf16[4,32,1024]{2,1,0:T(8,128)(2,1)S(1)} %collective-permute-done.29.refs_12_) | copy-start | bytes 786436
  202.1 18.0 %collective-permute-start.12 = (bf16[4,32,1024]{2,1,0:T(8,128)(2,1)}, bf16[4,32,1024]{2,1,0:T(8,128)(2,1)S(1)}, u32[]{:S(2)}, u32[]{:S(2)}) collective-permute-start(bf16[4,32,1024]{2,1,0:T(8,128)(2,1)} %get-tuple-element.33), channel_id=1, source_target_pairs={{0,2},{1,3},{2,0},{3,1},{4,6},{5,7},{6,4},{7,5},{8,10},{9,11},{10,... | collective-permute-start | bytes 786440 | tf_op jit(solution)/shard_map/ppermute | solution.py:325
  203.6 21.0 %copy-start.32 = (bf16[4,32,1024]{2,1,0:T(8,128)(2,1)}, bf16[4,32,1024]{2,1,0:T(8,128)(2,1)S(1)}, u32[]{:S(2)}) copy-start(bf16[4,32,1024]{2,1,0:T(8,128)(2,1)S(1)} %collective-permute-done.19.refs_6_) | copy-start | bytes 786436
  203.6 21.0 %collective-permute-start.13 = (bf16[4,32,1024]{2,1,0:T(8,128)(2,1)}, bf16[4,32,1024]{2,1,0:T(8,128)(2,1)S(1)}, u32[]{:S(2)}, u32[]{:S(2)}) collective-permute-start(bf16[4,32,1024]{2,1,0:T(8,128)(2,1)} %get-tuple-element.34), channel_id=1, source_target_pairs={{0,3},{1,2},{2,1},{3,0},{4,7},{5,6},{6,5},{7,4},{8,11},{9,10},{10,... | collective-permute-start | bytes 786440 | tf_op jit(solution)/shard_map/ppermute | solution.py:325
  208.9 15.7 %copy-start.36 = (bf16[4,32,1024]{2,1,0:T(8,128)(2,1)}, bf16[4,32,1024]{2,1,0:T(8,128)(2,1)S(1)}, u32[]{:S(2)}) copy-start(bf16[4,32,1024]{2,1,0:T(8,128)(2,1)S(1)} %collective-permute-done.20.refs_7_) | copy-start | bytes 786436
  (21 other events, 150.1 us)
where the time goes:
time: 266 us; the launch traced here: 261 us
  waiting for transfers between devices  117 us (44%)
  Pallas kernels  77.9 us (29%)
  starting transfers between devices  48.3 us (18%)
  other arithmetic  12.8 us (5%)
    ppermute x12, waiting for transfers between devices, on_device(): terms.append(lax.ppermute(send, 'lead', pairs))  56.7 us
    pallas_call x4, Pallas kernels, row_call(): pl.pallas_call(lambda *refs: row_kernel(n_space, *refs), out_shape=[jax.S...  42.8 us
    pallas_call x1, Pallas kernels, col_call(): pl.pallas_call(lambda *refs: col_kernel(n_chunks, n_space, *refs), out_sh...  35.1 us
    ppermute x4, waiting for transfers between devices, on_device(): got = lax.ppermute(sends[i], 'lead', swap)  29.9 us
    ppermute x24, waiting for transfers between devices, across(): return lax.ppermute(value, 'space', [(s, s ^ j) for s in range(n_space)])  29.4 us
    ppermute x12, starting transfers between devices, on_device(): terms.append(lax.ppermute(send, 'lead', pairs))  21 us
    ppermute x24, starting transfers between devices, across(): return lax.ppermute(value, 'space', [(s, s ^ j) for s in range(n_space)])  15.2 us
    ppermute x4, starting transfers between devices, on_device(): got = lax.ppermute(sends[i], 'lead', swap)  7.08 us
  transfers between devices with their start and end apart: 44, of which 17 were waited for; matrix products, arithmetic and copies ran while one was open for 3% of the time, Pallas kernels for 16%

commit v1 on v0

--- a/solution.py
+++ b/solution.py
@@ -87,15 +87,17 @@
             weights.append(jnp.exp2((s - top) * self.factor).astype(BF16))
         for e, (r, c) in zip(weights, self.units):
             both = dot(e, jnp.concatenate([v[r, c : c + self.head], ones], axis=1))
-            mix_ref[r, lane + c : lane + c + self.head] = (
+            mix_ref[r, pl.ds(lane + c, self.head)] = (
                 both[:, : self.head] / both[:, self.head :]
             ).astype(BF16)
 
     def project(self, x, w_ref, p):
         channels = w_ref.shape[0]
         first = p * self.pair
+        if not isinstance(p, int):
+            first = pl.multiple_of(first, self.pair)
         return [
-            dot(x, w_ref[:, c * channels + first : c * channels + first + self.pair]).astype(BF16)
+            dot(x, w_ref[:, pl.ds(c * channels + first, self.pair)]).astype(BF16)
             for c in range(3)
         ]
 
@@ -104,7 +106,7 @@
     mine_ref, other_ref, gain_ref, bias_ref = refs[:4]
     pieces = paired(refs[4 : 4 + 2 * n_space])
     outs = refs[4 + 2 * n_space : 4 + 3 * n_space]
-    h_ref, mix_ref, y_ref, w_ref, sems = refs[4 + 3 * n_space :]
+    h_ref, mix_ref, y_ref, qkv_ref, w_ref, sems = refs[4 + 3 * n_space :]
     half, width, channels = mine_ref.shape
     part = width // n_space
     space = place_ref[0]
@@ -123,16 +125,25 @@
     pairs = Pairs(2 * tokens, channels, None)
     for copy in groups[0]:
         copy.wait()
-    ahead = pairs.project(h_ref[...], w_ref, 0)
-    for p in range(HEADS // 2):
-        qkv = ahead
+    last = HEADS // 2 - 1
+    for c, value in enumerate(pairs.project(h_ref[...], w_ref, 0)):
+        qkv_ref[c] = value
+    for copy in groups[1]:
+        copy.wait()
+
+    def body(p, _):
+        qkv = [qkv_ref[c] for c in range(3)]
         scores = pairs.scores(qkv)
-        if p < 2:
-            for copy in groups[p + 1]:
-                copy.wait()
-        if p + 1 < HEADS // 2:
-            ahead = pairs.project(h_ref[...], w_ref, p + 1)
-        pairs.mix(scores, qkv, mix_ref, p * pairs.pair)
+        ahead = pairs.project(h_ref[...], w_ref, p + 1)
+        pairs.mix(scores, qkv, mix_ref, pl.multiple_of(p * pairs.pair, pairs.pair))
+        for c, value in enumerate(ahead):
+            qkv_ref[c] = value
+
+    lax.fori_loop(0, last, body, None)
+    for copy in groups[2]:
+        copy.wait()
+    qkv = [qkv_ref[c] for c in range(3)]
+    pairs.mix(pairs.scores(qkv), qkv, mix_ref, last * pairs.pair)
     y = dot(mix_ref[...], w_ref[:, 3 * channels :])
     y = (y + h_ref[...].astype(F32)).astype(BF16)
     for n in range(2):
@@ -160,6 +171,7 @@
             pltpu.VMEM((tokens, channels), BF16),
             pltpu.VMEM((tokens, channels), BF16),
             pltpu.VMEM((2 * half, width, channels), BF16),
+            pltpu.VMEM((3, tokens, 2 * channels // HEADS), BF16),
             *weight_scratch(channels, n_space),
         ],
         compiler_params=pltpu.CompilerParams(vmem_limit_bytes=60 << 20),
@@ -177,7 +189,7 @@
     chunks = refs[:count]
     gain_ref = refs[count]
     pieces = paired(refs[count + 1 : count + 1 + 2 * n_space])
-    o_ref, x_ref, n_ref, mix_ref, perm_ref, w_ref, sems = refs[count + 1 + 2 * n_space :]
+    o_ref, x_ref, n_ref, mix_ref, perm_ref, qkv_ref, w_ref, sems = refs[count + 1 + 2 * n_space :]
     rows, cols, channels = o_ref.shape
     deep = chunks[0].shape[0]
     space = place_ref[0]
@@ -203,42 +215,49 @@
     perm_ref[0] = ((here % rows) * each + here // rows == there).astype(BF16)
     perm_ref[1] = ((there % rows) * each + there // rows == here).astype(BF16)
 
+    def place_of(t):
+        return pl.ds(pl.multiple_of(t * each, each), each)
+
     def wide(t):
-        return x_ref[:, t * each : (t + 1) * each, :].reshape(tokens, channels)
+        return x_ref[:, place_of(t), :].reshape(tokens, channels)
 
     def prepare(t):
         x = wide(t)
         inverse = lax.rsqrt(jnp.mean(x * x, axis=-1, keepdims=True) + EPS)
         normed = (x * inverse * gain_ref[...]).astype(BF16)
-        n_ref[t % 2] = dot(perm_ref[0], normed).astype(BF16)
-
-    def finish(t):
+        n_ref[...] = dot(perm_ref[0], normed).astype(BF16)
+
+    def keep_ahead(values):
+        for c, value in enumerate(values):
+            qkv_ref[c] = value
+
+    last = HEADS // 2 - 1
+
+    def tile(t, _):
+        ahead = [qkv_ref[c] for c in range(3)]
+        for p in range(last + 1):
+            qkv = ahead
+            scores = pairs.scores(qkv)
+            if p < last:
+                ahead = pairs.project(n_ref[...], w_ref, p + 1)
+            else:
+                keep_ahead(pairs.project(n_ref[...], w_ref, 0))
+            if p == last - 1:
+                prepare(jnp.minimum(t + 1, tiles - 1))
+            pairs.mix(scores, qkv, mix_ref, p * pairs.pair)
         mixed = dot(perm_ref[1], mix_ref[...]).astype(BF16)
         y = wide(t) + dot(mixed, w_ref[:, 3 * channels :])
-        x_ref[:, t * each : (t + 1) * each, :] = y.reshape(rows, each, channels)
-        if (t + 1) * each % 16 == 0 or t + 1 == tiles:
-            at = slice((t + 1) * each - min(16, (t + 1) * each), (t + 1) * each)
-            o_ref[:, at, :] = x_ref[:, at, :].astype(BF16)
+        x_ref[:, place_of(t), :] = y.reshape(rows, each, channels)
 
     prepare(0)
     for copy in groups[0]:
         copy.wait()
-    ahead = pairs.project(n_ref[0], w_ref, 0)
+    keep_ahead(pairs.project(n_ref[...], w_ref, 0))
     for group in groups[1:]:
         for copy in group:
             copy.wait()
-    steps = [(t, p) for t in range(tiles) for p in range(HEADS // 2)]
-    for n, (t, p) in enumerate(steps):
-        qkv = ahead
-        scores = pairs.scores(qkv)
-        if n + 1 < len(steps):
-            after = steps[n + 1]
-            ahead = pairs.project(n_ref[after[0] % 2], w_ref, after[1])
-        if p == 1 and t + 1 < tiles:
-            prepare(t + 1)
-        pairs.mix(scores, qkv, mix_ref, p * pairs.pair)
-        if p + 1 == HEADS // 2:
-            finish(t)
+    lax.fori_loop(0, tiles, tile, None)
+    o_ref[...] = x_ref[...].astype(BF16)
 
 
 def col_call(place, chunks, gain, pieces):
@@ -257,9 +276,10 @@
         out_specs=vmem,
         scratch_shapes=[
             pltpu.VMEM((rows, cols, channels), F32),
-            pltpu.VMEM((2, tokens, channels), BF16),
+            pltpu.VMEM((tokens, channels), BF16),
             pltpu.VMEM((tokens, channels), BF16),
             pltpu.VMEM((2, tokens, tokens), BF16),
+            pltpu.VMEM((3, tokens, 2 * channels // HEADS), BF16),
             *weight_scratch(channels, n_space),
         ],
         compiler_params=pltpu.CompilerParams(vmem_limit_bytes=60 << 20),

time: 266 us -> 264 us (level); the launches traced: 261 us -> 263 us
  Pallas kernels: 77.9 us -> 80.8 us
  transfers between devices with their start and end apart: 44 -> 44, of which waited for: 17 -> 17; matrix products, arithmetic and copies ran while one was open for 3% -> 3% of each run, Pallas kernels for 16% -> 17%
where the time goes in v1:
time: 264 us; the launch traced here: 263 us
  waiting for transfers between devices  117 us (44%)
  Pallas kernels  80.8 us (31%)
  starting transfers between devices  48.3 us (18%)
  other arithmetic  12.8 us (5%)
    ppermute x12, waiting for transfers between devices, on_device(): terms.append(lax.ppermute(send, 'lead', pairs))  56.7 us
    pallas_call x4, Pallas kernels, row_call(): pl.pallas_call(lambda *refs: row_kernel(n_space, *refs), out_shape=[jax.S...  44.2 us
    pallas_call x1, Pallas kernels, col_call(): pl.pallas_call(lambda *refs: col_kernel(n_chunks, n_space, *refs), out_sh...  36.5 us
    ppermute x4, waiting for transfers between devices, on_device(): got = lax.ppermute(sends[i], 'lead', swap)  29.9 us
    ppermute x24, waiting for transfers between devices, across(): return lax.ppermute(value, 'space', [(s, s ^ j) for s in range(n_space)])  29.3 us
    ppermute x12, starting transfers between devices, on_device(): terms.append(lax.ppermute(send, 'lead', pairs))  21 us
    ppermute x24, starting transfers between devices, across(): return lax.ppermute(value, 'space', [(s, s ^ j) for s in range(n_space)])  15.2 us
    ppermute x4, starting transfers between devices, on_device(): got = lax.ppermute(sends[i], 'lead', swap)  7.08 us
  transfers between devices with their start and end apart: 44, of which 17 were waited for; matrix products, arithmetic and copies ran while one was open for 3% of the time, Pallas kernels for 17%

profile of v1, /device:TPU:0, one launch (start us, length us, event | category | flops | bytes accessed | tf_op | source)
XLA Modules:
  0.0 263.4 jit_solution(1916756017194076607)
XLA Ops:
  0.0 1.3 fusion
  1.3 3.2 %multiply_bitcast_fusion = (bf16[2,128,1024]{2,1,0:T(8,128)(2,1)S(1)}, bf16[2,128,1024]{2,1,0:T(8,128)(2,1)S(1)}, bf16[2,128,1024]{2,1,0:T(8,128)(2,1)S(1)}, bf1...) fusion(bf16[1,16,128,1024]{3,2,1,0:T(8,128)(2,1)} %param.10, ...), kind=kLoop, calls=%fused_computation.4 | loop fusion | flops 2097152 | bytes 8388642 | tf_op jit(solution)/shard_map/mul | solution.py:326
  4.5 3.0 %collective-permute-start.30 = (bf16[2,128,1024]{2,1,0:T(8,128)(2,1)S(1)}, bf16[2,128,1024]{2,1,0:T(8,128)(2,1)S(1)}, u32[]{:S(2)}, u32[]{:S(2)}) collective-permute-start(bf16[2,128,1024]{2,1,0:T(8,128)(2,1)S(1)} %get-tuple-element.48), channel_id=1, source_target_pairs={{0,4},{4,0},{8,12},{12,8},{16,20},{20,16},{24,28},{28,24},{1,5},{5... | collective-permute-start | bytes 1572872 | tf_op jit(solution)/shard_map/ppermute | solution.py:366
  7.5 1.5 collective-permute-start.8
  9.6 1.5 collective-permute-start.14
  11.1 9.2 %collective-permute-done.30 = bf16[2,128,1024]{2,1,0:T(8,128)(2,1)S(1)} collective-permute-done((bf16[2,128,1024]{2,1,0:T(8,128)(2,1)S(1)}, bf16[2,128,1024]{2,1,0:T(8,128)(2,1)S(1)}, u32[]{:S(2)}, u32[]{:S(2)}) %collective-permute-start.30) | collective-permute-done | bytes 524320 | tf_op jit(solution)/shard_map/ppermute | solution.py:366
  20.3 2.0 collective-permute-start
  22.3 1.6 collective-permute-start.41
  24.1 7.4 %collective-permute-done.22 = bf16[2,128,1024]{2,1,0:T(8,128)(2,1)S(1)} collective-permute-done((bf16[2,128,1024]{2,1,0:T(8,128)(2,1)S(1)}, bf16[2,128,1024]{2,1,0:T(8,128)(2,1)S(1)}, u32[]{:S(2)}, u32[]{:S(2)}) %collective-permute-start.22) | collective-permute-done | bytes 524320 | tf_op jit(solution)/shard_map/ppermute | solution.py:366
  31.5 4.0 %collective-permute-start.31 = (bf16[2,128,1024]{2,1,0:T(8,128)(2,1)S(1)}, bf16[2,128,1024]{2,1,0:T(8,128)(2,1)S(1)}, u32[]{:S(2)}, u32[]{:S(2)}) collective-permute-start(bf16[2,128,1024]{2,1,0:T(8,128)(2,1)S(1)} %add.156), channel_id=1, source_target_pairs={{24,16},{0,8},{28,20},{4,12},{25,17},{1,9},{29,21},{5,13},{26,18},... | collective-permute-start | bytes 1572872 | tf_op jit(solution)/shard_map/ppermute | solution.py:371
  35.9 6.9 %collective-permute-done.14 = bf16[2,128,1024]{2,1,0:T(8,128)(2,1)S(1)} collective-permute-done((bf16[2,128,1024]{2,1,0:T(8,128)(2,1)S(1)}, bf16[2,128,1024]{2,1,0:T(8,128)(2,1)S(1)}, u32[]{:S(2)}, u32[]{:S(2)}) %collective-permute-start.14) | collective-permute-done | bytes 524320 | tf_op jit(solution)/shard_map/ppermute | solution.py:366
  42.8 4.0 %collective-permute-start.23 = (bf16[2,128,1024]{2,1,0:T(8,128)(2,1)S(1)}, bf16[2,128,1024]{2,1,0:T(8,128)(2,1)S(1)}, u32[]{:S(2)}, u32[]{:S(2)}) collective-permute-start(bf16[2,128,1024]{2,1,0:T(8,128)(2,1)S(1)} %add.151), channel_id=1, source_target_pairs={{24,16},{0,8},{28,20},{4,12},{25,17},{1,9},{29,21},{5,13},{26,18},... | collective-permute-start | bytes 1572872 | tf_op jit(solution)/shard_map/ppermute | solution.py:371
  46.8 6.3 %collective-permute-done = bf16[2,128,1024]{2,1,0:T(8,128)(2,1)S(1)} collective-permute-done((bf16[2,128,1024]{2,1,0:T(8,128)(2,1)S(1)}, bf16[2,128,1024]{2,1,0:T(8,128)(2,1)S(1)}, u32[]{:S(2)}, u32[]{:S(2)}) %collective-permute-start) | collective-permute-done | bytes 524320 | tf_op jit(solution)/shard_map/ppermute | solution.py:366
  53.1 1.8 collective-permute-start.7
  55.1 3.5 %collective-permute-start.15 = (bf16[2,128,1024]{2,1,0:T(8,128)(2,1)S(1)}, bf16[2,128,1024]{2,1,0:T(8,128)(2,1)S(1)}, u32[]{:S(2)}, u32[]{:S(2)}) collective-permute-start(bf16[2,128,1024]{2,1,0:T(8,128)(2,1)S(1)} %add.146), channel_id=1, source_target_pairs={{24,16},{0,8},{28,20},{4,12},{25,17},{1,9},{29,21},{5,13},{26,18},... | collective-permute-start | bytes 1572872 | tf_op jit(solution)/shard_map/ppermute | solution.py:371
  59.2 1.3 collective-permute-start.1
  60.5 0.7 collective-permute-start.32
  61.4 9.5 %collective-permute-done.15 = bf16[2,128,1024]{2,1,0:T(8,128)(2,1)S(1)} collective-permute-done((bf16[2,128,1024]{2,1,0:T(8,128)(2,1)S(1)}, bf16[2,128,1024]{2,1,0:T(8,128)(2,1)S(1)}, u32[]{:S(2)}, u32[]{:S(2)}) %collective-permute-start.15) | collective-permute-done | bytes 524320 | tf_op jit(solution)/shard_map/ppermute | solution.py:371
  70.9 0.7 collective-permute-start.24
  71.8 0.7 collective-permute-start.16
  72.5 7.4 %collective-permute-done.1 = bf16[2,128,1024]{2,1,0:T(8,128)(2,1)S(1)} collective-permute-done((bf16[2,128,1024]{2,1,0:T(8,128)(2,1)S(1)}, bf16[2,128,1024]{2,1,0:T(8,128)(2,1)S(1)}, u32[]{:S(2)}, u32[]{:S(2)}) %collective-permute-start.1) | collective-permute-done | bytes 524320 | tf_op jit(solution)/shard_map/ppermute | solution.py:371
  80.7 0.7 collective-permute-start.2
  81.4 1.0 add.159
  82.4 1.3 collective-permute-start.33
  83.7 7.0 %collective-permute-done.7.refs_9_ = bf16[256,3072]{1,0:T(8,128)(2,1)} collective-permute-done((bf16[256,3072]{1,0:T(8,128)(2,1)}, bf16[256,3072]{1,0:T(8,128)(2,1)}, u32[]{:S(2)}, u32[]{:S(2)}) %collective-permute-start.7) | collective-permute-done | bytes 1572896 | tf_op jit(solution)/shard_map/ppermute | solution.py:345
  90.7 1.0 add.154
  91.8 0.8 copy-done.2
  92.6 1.3 collective-permute-start.25
  94.5 0.6 pad_add_fusion.refs_0_
  95.1 1.4 dynamic-slice_add_fusion
  96.9 13.1 %collective-permute-done.33 = bf16[2,128,1024]{2,1,0:T(8,128)(2,1)} collective-permute-done((bf16[2,128,1024]{2,1,0:T(8,128)(2,1)}, bf16[2,128,1024]{2,1,0:T(8,128)(2,1)}, u32[]{:S(2)}, u32[]{:S(2)}) %collective-permute-start.33) | collective-permute-done | bytes 524320 | tf_op jit(solution)/shard_map/ppermute | solution.py:371
  110.0 1.3 collective-permute-start.17
  111.3 1.1 add_add_fusion.refs_1_
  112.5 12.4 %collective-permute-done.25 = bf16[2,128,1024]{2,1,0:T(8,128)(2,1)} collective-permute-done((bf16[2,128,1024]{2,1,0:T(8,128)(2,1)}, bf16[2,128,1024]{2,1,0:T(8,128)(2,1)}, u32[]{:S(2)}, u32[]{:S(2)}) %collective-permute-start.25) | collective-permute-done | bytes 524320 | tf_op jit(solution)/shard_map/ppermute | solution.py:371
  124.9 1.5 collective-permute-start.3
  126.4 1.1 add_add_fusion.1.refs_1_
  128.1 7.9 %collective-permute-done.17 = bf16[2,128,1024]{2,1,0:T(8,128)(2,1)S(1)} collective-permute-done((bf16[2,128,1024]{2,1,0:T(8,128)(2,1)S(1)}, bf16[2,128,1024]{2,1,0:T(8,128)(2,1)S(1)}, u32[]{:S(2)}, u32[]{:S(2)}) %collective-permute-start.17) | collective-permute-done | bytes 524320 | tf_op jit(solution)/shard_map/ppermute | solution.py:371
  136.0 1.5 collective-permute-start.34
  137.6 6.4 %collective-permute-done.3 = bf16[2,128,1024]{2,1,0:T(8,128)(2,1)S(1)} collective-permute-done((bf16[2,128,1024]{2,1,0:T(8,128)(2,1)S(1)}, bf16[2,128,1024]{2,1,0:T(8,128)(2,1)S(1)}, u32[]{:S(2)}, u32[]{:S(2)}) %collective-permute-start.3) | collective-permute-done | bytes 524320 | tf_op jit(solution)/shard_map/ppermute | solution.py:371
  144.0 1.5 collective-permute-start.26
  145.6 1.3 collective-permute-done.34.refs_2_
  147.0 0.8 copy-done.22
  147.8 1.5 collective-permute-start.18
  149.3 11.0 %row_attention.7 = (bf16[4,32,1024]{2,1,0:T(8,128)(2,1)}, bf16[4,32,1024]{2,1,0:T(8,128)(2,1)}, bf16[4,32,1024]{2,1,0:T(8,128)(2,1)}, bf16[4,32,1024]{2,1,0:T(8,128)(2,1)}) custom-call(s32[2]{0:T(128)} %pad_add_fusion.refs_0_, bf16[2,128,1024]{2,1,0:T(8,128)(2,1)} %copy-done.10, bf16[2,128,1024]{2,1,0:T(8,128)(2,1)} %copy-done.22, ...), custom_call_target="tpu_custom_call" | custom-call | flops 4563402752 | bytes 10485760 | tf_op jit(solution)/shard_map/row_attention/pallas_call | solution.py:163
  160.3 0.6 collective-permute-start.4
  160.9 11.0 %row_attention.6 = (bf16[4,32,1024]{2,1,0:T(8,128)(2,1)}, bf16[4,32,1024]{2,1,0:T(8,128)(2,1)}, bf16[4,32,1024]{2,1,0:T(8,128)(2,1)}, bf16[4,32,1024]{2,1,0:T(8,128)(2,1)}) custom-call(s32[2]{0:T(128)} %pad_add_fusion.refs_0_, bf16[2,128,1024]{2,1,0:T(8,128)(2,1)} %copy-done.9, bf16[2,128,1024]{2,1,0:T(8,128)(2,1)} %collective-permute-done.26.refs_2_, ...), custom_call_target="tpu_custom_call" | custom-call | flops 4563402752 | bytes 10485760 | tf_op jit(solution)/shard_map/row_attention/pallas_call | solution.py:163
  172.9 11.2 %row_attention.5 = (bf16[4,32,1024]{2,1,0:T(8,128)(2,1)}, bf16[4,32,1024]{2,1,0:T(8,128)(2,1)}, bf16[4,32,1024]{2,1,0:T(8,128)(2,1)}, bf16[4,32,1024]{2,1,0:T(8,128)(2,1)}) custom-call(s32[2]{0:T(128)} %pad_add_fusion.refs_0_, bf16[2,128,1024]{2,1,0:T(8,128)(2,1)} %copy-done.11, bf16[2,128,1024]{2,1,0:T(8,128)(2,1)} %copy-done.21, ...), custom_call_target="tpu_custom_call" | custom-call | flops 4563402752 | bytes 10485760 | tf_op jit(solution)/shard_map/row_attention/pallas_call | solution.py:163
  184.2 1.1 collective-permute-start.37
  185.7 0.8 collective-permute-start.28
  186.5 0.8 collective-permute-start.29
  187.3 0.7 collective-permute-start.19
  188.0 11.0 %row_attention.4 = (bf16[4,32,1024]{2,1,0:T(8,128)(2,1)}, bf16[4,32,1024]{2,1,0:T(8,128)(2,1)}, bf16[4,32,1024]{2,1,0:T(8,128)(2,1)}, bf16[4,32,1024]{2,1,0:T(8,128)(2,1)}) custom-call(s32[2]{0:T(128)} %pad_add_fusion.refs_0_, bf16[2,128,1024]{2,1,0:T(8,128)(2,1)} %copy-done.8, bf16[2,128,1024]{2,1,0:T(8,128)(2,1)} %copy-done.20, ...), custom_call_target="tpu_custom_call" | custom-call | flops 4563402752 | bytes 10485760 | tf_op jit(solution)/shard_map/row_attention/pallas_call | solution.py:163
  199.0 0.8 collective-permute-start.20
  199.9 0.8 collective-permute-start.21
  200.7 0.6 collective-permute-start.11
  201.3 2.2 collective-permute-done.29.refs_12_
  203.5 1.5 collective-permute-start.12
  205.0 0.9 collective-permute-start.13
  205.8 4.4 %collective-permute-done.20.refs_7_ = bf16[4,32,1024]{2,1,0:T(8,128)(2,1)S(1)} collective-permute-done((bf16[4,32,1024]{2,1,0:T(8,128)(2,1)S(1)}, bf16[4,32,1024]{2,1,0:T(8,128)(2,1)S(1)}, u32[]{:S(2)}, u32[]{:S(2)}) %collective-permute-start.20) | collective-permute-done | bytes 262176 | tf_op jit(solution)/shard_map/ppermute | solution.py:345
  210.3 4.4 %collective-permute-done.21.refs_8_ = bf16[4,32,1024]{2,1,0:T(8,128)(2,1)S(1)} collective-permute-done((bf16[4,32,1024]{2,1,0:T(8,128)(2,1)S(1)}, bf16[4,32,1024]{2,1,0:T(8,128)(2,1)S(1)}, u32[]{:S(2)}, u32[]{:S(2)}) %collective-permute-start.21) | collective-permute-done | bytes 262176 | tf_op jit(solution)/shard_map/ppermute | solution.py:345
  214.7 6.8 %collective-permute-done.12.refs_3_ = bf16[4,32,1024]{2,1,0:T(8,128)(2,1)S(1)} collective-permute-done((bf16[4,32,1024]{2,1,0:T(8,128)(2,1)}, bf16[4,32,1024]{2,1,0:T(8,128)(2,1)S(1)}, u32[]{:S(2)}, u32[]{:S(2)}) %collective-permute-start.12) | collective-permute-done | bytes 262176 | tf_op jit(solution)/shard_map/ppermute | solution.py:345
  221.5 4.4 %collective-permute-done.13.refs_4_ = bf16[4,32,1024]{2,1,0:T(8,128)(2,1)S(1)} collective-permute-done((bf16[4,32,1024]{2,1,0:T(8,128)(2,1)}, bf16[4,32,1024]{2,1,0:T(8,128)(2,1)S(1)}, u32[]{:S(2)}, u32[]{:S(2)}) %collective-permute-start.13) | collective-permute-done | bytes 262176 | tf_op jit(solution)/shard_map/ppermute | solution.py:345
  226.0 0.6 copy-done.40
  226.6 36.5 %col_attention.1 = bf16[64,32,1024]{2,1,0:T(8,128)(2,1)} custom-call(s32[2]{0:T(128)} %pad_add_fusion.refs_0_, bf16[4,32,1024]{2,1,0:T(8,128)(2,1)} %get-tuple-element.31.refs_1_, bf16[4,32,1024]{2,1,0:T(8,128)(2,1)} %copy-done.38, bf16[4,32,1024]{2,1,0:T(8,128)(2,1)} %copy-done.39, bf16[4,32,1024]{2,1,0:T(8,128)(2,1)} %copy-done.40, ...), custom_call_target="tpu_custom_call" | custom-call | flops 17716740096 | bytes 16777216 | tf_op jit(solution)/shard_map/col_attention/pallas_call | solution.py:270
  (131 shorter events, 5.4 us)
Async XLA Ops:
  1.3 21.0 %copy-start.13 = (bf16[256,1024]{1,0:T(8,128)(2,1)S(1)}, bf16[256,1024]{1,0:T(8,128)(2,1)}, u32[]{:S(2)}) copy-start(bf16[256,1024]{1,0:T(8,128)(2,1)} %refs_19_.1) | copy-start | bytes 1572868
  4.5 15.8 %collective-permute-start.30 = (bf16[2,128,1024]{2,1,0:T(8,128)(2,1)S(1)}, bf16[2,128,1024]{2,1,0:T(8,128)(2,1)S(1)}, u32[]{:S(2)}, u32[]{:S(2)}) collective-permute-start(bf16[2,128,1024]{2,1,0:T(8,128)(2,1)S(1)} %get-tuple-element.48), channel_id=1, source_target_pairs={{0,4},{4,0},{8,12},{12,8},{16,20},{20,16},{24,28},{28,24},{1,5},{5... | collective-permute-start | bytes 1572872 | tf_op jit(solution)/shard_map/ppermute | solution.py:366
  7.5 14.8 %collective-permute-start.8 = (bf16[256,1024]{1,0:T(8,128)(2,1)S(1)}, bf16[256,1024]{1,0:T(8,128)(2,1)S(1)}, u32[]{:S(2)}, u32[]{:S(2)}) collective-permute-start(bf16[256,1024]{1,0:T(8,128)(2,1)S(1)} %copy-done.12), channel_id=1, source_target_pairs={{0,2},{1,3},{2,0},{3,1},{4,6},{5,7},{6,4},{7,5},{8,10},{9,11},{10,... | collective-permute-start | bytes 1572872 | tf_op jit(solution)/shard_map/ppermute | solution.py:345
  9.0 22.5 %collective-permute-start.22 = (bf16[2,128,1024]{2,1,0:T(8,128)(2,1)S(1)}, bf16[2,128,1024]{2,1,0:T(8,128)(2,1)S(1)}, u32[]{:S(2)}, u32[]{:S(2)}) collective-permute-start(bf16[2,128,1024]{2,1,0:T(8,128)(2,1)S(1)} %get-tuple-element.42), channel_id=1, source_target_pairs={{0,4},{4,0},{8,12},{12,8},{16,20},{20,16},{24,28},{28,24},{1,5},{5... | collective-permute-start | bytes 1572872 | tf_op jit(solution)/shard_map/ppermute | solution.py:366
  9.6 26.2 %collective-permute-start.6 = (bf16[256,1024]{1,0:T(8,128)(2,1)S(1)}, bf16[256,1024]{1,0:T(8,128)(2,1)S(1)}, u32[]{:S(2)}, u32[]{:S(2)}) collective-permute-start(bf16[256,1024]{1,0:T(8,128)(2,1)S(1)} %copy-done.12), channel_id=1, source_target_pairs={{0,1},{1,0},{2,3},{3,2},{4,5},{5,4},{6,7},{7,6},{8,9},{9,8},{10,11... | collective-permute-start | bytes 1572872 | tf_op jit(solution)/shard_map/ppermute | solution.py:345
  9.6 33.2 %collective-permute-start.14 = (bf16[2,128,1024]{2,1,0:T(8,128)(2,1)S(1)}, bf16[2,128,1024]{2,1,0:T(8,128)(2,1)S(1)}, u32[]{:S(2)}, u32[]{:S(2)}) collective-permute-start(bf16[2,128,1024]{2,1,0:T(8,128)(2,1)S(1)} %get-tuple-element.36), channel_id=1, source_target_pairs={{0,4},{4,0},{8,12},{12,8},{16,20},{20,16},{24,28},{28,24},{1,5},{5... | collective-permute-start | bytes 1572872 | tf_op jit(solution)/shard_map/ppermute | solution.py:366
  20.3 32.9 %collective-permute-start = (bf16[2,128,1024]{2,1,0:T(8,128)(2,1)S(1)}, bf16[2,128,1024]{2,1,0:T(8,128)(2,1)S(1)}, u32[]{:S(2)}, u32[]{:S(2)}) collective-permute-start(bf16[2,128,1024]{2,1,0:T(8,128)(2,1)S(1)} %get-tuple-element.30), channel_id=1, source_target_pairs={{0,4},{4,0},{8,12},{12,8},{16,20},{20,16},{24,28},{28,24},{1,5},{5... | collective-permute-start | bytes 1572872 | tf_op jit(solution)/shard_map/ppermute | solution.py:366
  22.3 36.3 %copy-start.16 = (bf16[256,1024]{1,0:T(8,128)(2,1)}, bf16[256,1024]{1,0:T(8,128)(2,1)S(1)}, u32[]{:S(2)}) copy-start(bf16[256,1024]{1,0:T(8,128)(2,1)S(1)} %collective-permute-done.8.refs_10_) | copy-start | bytes 1572868
  22.3 32.8 %collective-permute-start.41 = (bf16[256,1024]{1,0:T(8,128)(2,1)S(1)}, bf16[256,1024]{1,0:T(8,128)(2,1)S(1)}, u32[]{:S(2)}, u32[]{:S(2)}) collective-permute-start(bf16[256,1024]{1,0:T(8,128)(2,1)S(1)} %copy-done.13), channel_id=1, source_target_pairs={{0,2},{1,3},{2,0},{3,1},{4,6},{5,7},{6,4},{7,5},{8,10},{9,11},{10,... | collective-permute-start | bytes 1572872 | tf_op jit(solution)/shard_map/ppermute | solution.py:345
  31.5 27.1 %collective-permute-start.31 = (bf16[2,128,1024]{2,1,0:T(8,128)(2,1)S(1)}, bf16[2,128,1024]{2,1,0:T(8,128)(2,1)S(1)}, u32[]{:S(2)}, u32[]{:S(2)}) collective-permute-start(bf16[2,128,1024]{2,1,0:T(8,128)(2,1)S(1)} %add.156), channel_id=1, source_target_pairs={{24,16},{0,8},{28,20},{4,12},{25,17},{1,9},{29,21},{5,13},{26,18},... | collective-permute-start | bytes 1572872 | tf_op jit(solution)/shard_map/ppermute | solution.py:371
  35.8 23.2 %copy-start.17 = (bf16[256,1024]{1,0:T(8,128)(2,1)}, bf16[256,1024]{1,0:T(8,128)(2,1)S(1)}, u32[]{:S(2)}) copy-start(bf16[256,1024]{1,0:T(8,128)(2,1)S(1)} %collective-permute-done.6.refs_8_) | copy-start | bytes 1572868
  35.8 23.4 %collective-permute-start.39 = (bf16[256,1024]{1,0:T(8,128)(2,1)S(1)}, bf16[256,1024]{1,0:T(8,128)(2,1)}, u32[]{:S(2)}, u32[]{:S(2)}) collective-permute-start(bf16[256,1024]{1,0:T(8,128)(2,1)S(1)} %copy-done.13), channel_id=1, source_target_pairs={{0,1},{1,0},{2,3},{3,2},{4,5},{5,4},{6,7},{7,6},{8,9},{9,8},{10,11... | collective-permute-start | bytes 1572872 | tf_op jit(solution)/shard_map/ppermute | solution.py:345
  42.8 17.8 %collective-permute-start.23 = (bf16[2,128,1024]{2,1,0:T(8,128)(2,1)S(1)}, bf16[2,128,1024]{2,1,0:T(8,128)(2,1)S(1)}, u32[]{:S(2)}, u32[]{:S(2)}) collective-permute-start(bf16[2,128,1024]{2,1,0:T(8,128)(2,1)S(1)} %add.151), channel_id=1, source_target_pairs={{24,16},{0,8},{28,20},{4,12},{25,17},{1,9},{29,21},{5,13},{26,18},... | collective-permute-start | bytes 1572872 | tf_op jit(solution)/shard_map/ppermute | solution.py:371
  53.1 37.6 %collective-permute-start.7 = (bf16[256,3072]{1,0:T(8,128)(2,1)}, bf16[256,3072]{1,0:T(8,128)(2,1)}, u32[]{:S(2)}, u32[]{:S(2)}) collective-permute-start(bf16[256,3072]{1,0:T(8,128)(2,1)} %refs_5_.7), channel_id=1, source_target_pairs={{0,2},{1,3},{2,0},{3,1},{4,6},{5,7},{6,4},{7,5},{8,10},{9,11},{10,... | collective-permute-start | bytes 4718600 | tf_op jit(solution)/shard_map/ppermute | solution.py:345
  55.1 15.8 %collective-permute-start.15 = (bf16[2,128,1024]{2,1,0:T(8,128)(2,1)S(1)}, bf16[2,128,1024]{2,1,0:T(8,128)(2,1)S(1)}, u32[]{:S(2)}, u32[]{:S(2)}) collective-permute-start(bf16[2,128,1024]{2,1,0:T(8,128)(2,1)S(1)} %add.146), channel_id=1, source_target_pairs={{24,16},{0,8},{28,20},{4,12},{25,17},{1,9},{29,21},{5,13},{26,18},... | collective-permute-start | bytes 1572872 | tf_op jit(solution)/shard_map/ppermute | solution.py:371
  58.7 13.1 %collective-permute-start.10 = (bf16[256,1024]{1,0:T(8,128)(2,1)S(1)}, bf16[256,1024]{1,0:T(8,128)(2,1)S(1)}, u32[]{:S(2)}, u32[]{:S(2)}) collective-permute-start(bf16[256,1024]{1,0:T(8,128)(2,1)S(1)} %collective-permute-done.8.refs_10_), channel_id=1, source_target_pairs={{0,1},{1,0},{2,3},{3,2},{4,5},{5,4},{6,7},{7,6},{8,9},{9,8},{10,11... | collective-permute-start | bytes 1572872 | tf_op jit(solution)/shard_map/ppermute | solution.py:345
  59.2 20.7 %collective-permute-start.1 = (bf16[2,128,1024]{2,1,0:T(8,128)(2,1)S(1)}, bf16[2,128,1024]{2,1,0:T(8,128)(2,1)S(1)}, u32[]{:S(2)}, u32[]{:S(2)}) collective-permute-start(bf16[2,128,1024]{2,1,0:T(8,128)(2,1)S(1)} %add.138), channel_id=1, source_target_pairs={{24,16},{0,8},{28,20},{4,12},{25,17},{1,9},{29,21},{5,13},{26,18},... | collective-permute-start | bytes 1572872 | tf_op jit(solution)/shard_map/ppermute | solution.py:371
  60.5 19.4 %collective-permute-start.32 = (bf16[2,128,1024]{2,1,0:T(8,128)(2,1)S(1)}, bf16[2,128,1024]{2,1,0:T(8,128)(2,1)S(1)}, u32[]{:S(2)}, u32[]{:S(2)}) collective-permute-start(bf16[2,128,1024]{2,1,0:T(8,128)(2,1)S(1)} %add.157), channel_id=1, source_target_pairs={{16,8},{8,16},{20,12},{12,20},{17,9},{9,17},{21,13},{13,21},{18,10... | collective-permute-start | bytes 1572872 | tf_op jit(solution)/shard_map/ppermute | solution.py:371
  61.4 19.2 %copy-start = (bf16[2,128,1024]{2,1,0:T(8,128)(2,1)}, bf16[2,128,1024]{2,1,0:T(8,128)(2,1)S(1)}, u32[]{:S(2)}) copy-start(bf16[2,128,1024]{2,1,0:T(8,128)(2,1)S(1)} %add.152) | copy-start | bytes 1572868
  70.9 9.8 %collective-permute-start.24 = (bf16[2,128,1024]{2,1,0:T(8,128)(2,1)S(1)}, bf16[2,128,1024]{2,1,0:T(8,128)(2,1)S(1)}, u32[]{:S(2)}, u32[]{:S(2)}) collective-permute-start(bf16[2,128,1024]{2,1,0:T(8,128)(2,1)S(1)} %add.152), channel_id=1, source_target_pairs={{16,8},{8,16},{20,12},{12,20},{17,9},{9,17},{21,13},{13,21},{18,10... | collective-permute-start | bytes 1572872 | tf_op jit(solution)/shard_map/ppermute | solution.py:371
  71.8 10.6 %collective-permute-start.16 = (bf16[2,128,1024]{2,1,0:T(8,128)(2,1)S(1)}, bf16[2,128,1024]{2,1,0:T(8,128)(2,1)S(1)}, u32[]{:S(2)}, u32[]{:S(2)}) collective-permute-start(bf16[2,128,1024]{2,1,0:T(8,128)(2,1)S(1)} %add.147), channel_id=1, source_target_pairs={{16,8},{8,16},{20,12},{12,20},{17,9},{9,17},{21,13},{13,21},{18,10... | collective-permute-start | bytes 1572872 | tf_op jit(solution)/shard_map/ppermute | solution.py:371
  79.9 47.7 %collective-permute-start.5 = (bf16[256,3072]{1,0:T(8,128)(2,1)}, bf16[256,3072]{1,0:T(8,128)(2,1)}, u32[]{:S(2)}, u32[]{:S(2)}) collective-permute-start(bf16[256,3072]{1,0:T(8,128)(2,1)} %refs_5_.7), channel_id=1, source_target_pairs={{0,1},{1,0},{2,3},{3,2},{4,5},{5,4},{6,7},{7,6},{8,9},{9,8},{10,11... | collective-permute-start | bytes 4718600 | tf_op jit(solution)/shard_map/ppermute | solution.py:345
  79.9 47.7 %collective-permute-start.40 = (bf16[256,3072]{1,0:T(8,128)(2,1)}, bf16[256,3072]{1,0:T(8,128)(2,1)}, u32[]{:S(2)}, u32[]{:S(2)}) collective-permute-start(bf16[256,3072]{1,0:T(8,128)(2,1)} %refs_18_.1), channel_id=1, source_target_pairs={{0,2},{1,3},{2,0},{3,1},{4,6},{5,7},{6,4},{7,5},{8,10},{9,11},{10,... | collective-permute-start | bytes 4718600 | tf_op jit(solution)/shard_map/ppermute | solution.py:345
  80.7 11.1 %collective-permute-start.2 = (bf16[2,128,1024]{2,1,0:T(8,128)(2,1)S(1)}, bf16[2,128,1024]{2,1,0:T(8,128)(2,1)S(1)}, u32[]{:S(2)}, u32[]{:S(2)}) collective-permute-start(bf16[2,128,1024]{2,1,0:T(8,128)(2,1)S(1)} %add.139), channel_id=1, source_target_pairs={{16,8},{8,16},{20,12},{12,20},{17,9},{9,17},{21,13},{13,21},{18,10... | collective-permute-start | bytes 1572872 | tf_op jit(solution)/shard_map/ppermute | solution.py:371
  82.4 27.6 %collective-permute-start.33 = (bf16[2,128,1024]{2,1,0:T(8,128)(2,1)}, bf16[2,128,1024]{2,1,0:T(8,128)(2,1)}, u32[]{:S(2)}, u32[]{:S(2)}) collective-permute-start(bf16[2,128,1024]{2,1,0:T(8,128)(2,1)} %add.159), channel_id=1, source_target_pairs={{8,0},{16,24},{12,4},{20,28},{9,1},{17,25},{13,5},{21,29},{10,2},{... | collective-permute-start | bytes 1572872 | tf_op jit(solution)/shard_map/ppermute | solution.py:371
  90.7 57.0 %collective-permute-start.9 = (bf16[256,3072]{1,0:T(8,128)(2,1)}, bf16[256,3072]{1,0:T(8,128)(2,1)}, u32[]{:S(2)}, u32[]{:S(2)}) collective-permute-start(bf16[256,3072]{1,0:T(8,128)(2,1)} %collective-permute-done.7.refs_9_), channel_id=1, source_target_pairs={{0,1},{1,0},{2,3},{3,2},{4,5},{5,4},{6,7},{7,6},{8,9},{9,8},{10,11... | collective-permute-start | bytes 4718600 | tf_op jit(solution)/shard_map/ppermute | solution.py:345
  92.6 32.4 %collective-permute-start.25 = (bf16[2,128,1024]{2,1,0:T(8,128)(2,1)}, bf16[2,128,1024]{2,1,0:T(8,128)(2,1)}, u32[]{:S(2)}, u32[]{:S(2)}) collective-permute-start(bf16[2,128,1024]{2,1,0:T(8,128)(2,1)} %add.154), channel_id=1, source_target_pairs={{8,0},{16,24},{12,4},{20,28},{9,1},{17,25},{13,5},{21,29},{10,2},{... | collective-permute-start | bytes 1572872 | tf_op jit(solution)/shard_map/ppermute | solution.py:371
  96.5 14.8 %copy-start.7 = (bf16[2,128,1024]{2,1,0:T(8,128)(2,1)S(1)}, bf16[2,128,1024]{2,1,0:T(8,128)(2,1)}, u32[]{:S(2)}) copy-start(bf16[2,128,1024]{2,1,0:T(8,128)(2,1)} %copy-done.6) | copy-start | bytes 1572868
  96.7 29.7 %copy-start.1 = (bf16[2,128,1024]{2,1,0:T(8,128)(2,1)S(1)}, bf16[2,128,1024]{2,1,0:T(8,128)(2,1)}, u32[]{:S(2)}) copy-start(bf16[2,128,1024]{2,1,0:T(8,128)(2,1)} %copy-done) | copy-start | bytes 1572868
  96.7 29.7 %copy-start.5 = (bf16[2,128,1024]{2,1,0:T(8,128)(2,1)S(1)}, bf16[2,128,1024]{2,1,0:T(8,128)(2,1)}, u32[]{:S(2)}) copy-start(bf16[2,128,1024]{2,1,0:T(8,128)(2,1)} %copy-done.4) | copy-start | bytes 1572868
  110.0 26.0 %collective-permute-start.17 = (bf16[2,128,1024]{2,1,0:T(8,128)(2,1)S(1)}, bf16[2,128,1024]{2,1,0:T(8,128)(2,1)S(1)}, u32[]{:S(2)}, u32[]{:S(2)}) collective-permute-start(bf16[2,128,1024]{2,1,0:T(8,128)(2,1)S(1)} %add.149), channel_id=1, source_target_pairs={{8,0},{16,24},{12,4},{20,28},{9,1},{17,25},{13,5},{21,29},{10,2},{... | collective-permute-start | bytes 1572872 | tf_op jit(solution)/shard_map/ppermute | solution.py:371
  112.5 25.2 %copy-start.10 = (bf16[2,128,1024]{2,1,0:T(8,128)(2,1)}, bf16[2,128,1024]{2,1,0:T(8,128)(2,1)S(1)}, u32[]{:S(2)}) copy-start(bf16[2,128,1024]{2,1,0:T(8,128)(2,1)S(1)} %add_add_fusion.refs_1_) | copy-start | bytes 1572868
  124.9 19.1 %collective-permute-start.3 = (bf16[2,128,1024]{2,1,0:T(8,128)(2,1)S(1)}, bf16[2,128,1024]{2,1,0:T(8,128)(2,1)S(1)}, u32[]{:S(2)}, u32[]{:S(2)}) collective-permute-start(bf16[2,128,1024]{2,1,0:T(8,128)(2,1)S(1)} %add.141), channel_id=1, source_target_pairs={{8,0},{16,24},{12,4},{20,28},{9,1},{17,25},{13,5},{21,29},{10,2},{... | collective-permute-start | bytes 1572872 | tf_op jit(solution)/shard_map/ppermute | solution.py:371
  127.5 18.1 %copy-start.9 = (bf16[2,128,1024]{2,1,0:T(8,128)(2,1)}, bf16[2,128,1024]{2,1,0:T(8,128)(2,1)S(1)}, u32[]{:S(2)}) copy-start(bf16[2,128,1024]{2,1,0:T(8,128)(2,1)S(1)} %add_add_fusion.1.refs_1_) | copy-start | bytes 1572868
  127.5 56.6 %collective-permute-start.38 = (bf16[256,3072]{1,0:T(8,128)(2,1)}, bf16[256,3072]{1,0:T(8,128)(2,1)}, u32[]{:S(2)}, u32[]{:S(2)}) collective-permute-start(bf16[256,3072]{1,0:T(8,128)(2,1)} %refs_18_.1), channel_id=1, source_target_pairs={{0,1},{1,0},{2,3},{3,2},{4,5},{5,4},{6,7},{7,6},{8,9},{9,8},{10,11... | collective-permute-start | bytes 4718600 | tf_op jit(solution)/shard_map/ppermute | solution.py:345
  127.6 58.1 %collective-permute-start.42 = (bf16[256,3072]{1,0:T(8,128)(2,1)}, bf16[256,3072]{1,0:T(8,128)(2,1)}, u32[]{:S(2)}, u32[]{:S(2)}) collective-permute-start(bf16[256,3072]{1,0:T(8,128)(2,1)} %collective-permute-done.40.refs_22_), channel_id=1, source_target_pairs={{0,1},{1,0},{2,3},{3,2},{4,5},{5,4},{6,7},{7,6},{8,9},{9,8},{10,11... | collective-permute-start | bytes 4718600 | tf_op jit(solution)/shard_map/ppermute | solution.py:345
  136.0 10.9 %collective-permute-start.34 = (bf16[2,128,1024]{2,1,0:T(8,128)(2,1)S(1)}, bf16[2,128,1024]{2,1,0:T(8,128)(2,1)S(1)}, u32[]{:S(2)}, u32[]{:S(2)}) collective-permute-start(bf16[2,128,1024]{2,1,0:T(8,128)(2,1)S(1)} %add_add_fusion.refs_1_), channel_id=1, source_target_pairs={{0,4},{4,0},{8,12},{12,8},{16,20},{20,16},{24,28},{28,24},{1,5},{5... | collective-permute-start | bytes 1572872 | tf_op jit(solution)/shard_map/ppermute | solution.py:375
  137.6 22.6 %copy-start.11 = (bf16[2,128,1024]{2,1,0:T(8,128)(2,1)}, bf16[2,128,1024]{2,1,0:T(8,128)(2,1)S(1)}, u32[]{:S(2)}) copy-start(bf16[2,128,1024]{2,1,0:T(8,128)(2,1)S(1)} %add_add_fusion.2.refs_1_) | copy-start | bytes 1572868
  144.0 16.2 %collective-permute-start.26 = (bf16[2,128,1024]{2,1,0:T(8,128)(2,1)S(1)}, bf16[2,128,1024]{2,1,0:T(8,128)(2,1)}, u32[]{:S(2)}, u32[]{:S(2)}) collective-permute-start(bf16[2,128,1024]{2,1,0:T(8,128)(2,1)S(1)} %add_add_fusion.1.refs_1_), channel_id=1, source_target_pairs={{0,4},{4,0},{8,12},{12,8},{16,20},{20,16},{24,28},{28,24},{1,5},{5... | collective-permute-start | bytes 1572872 | tf_op jit(solution)/shard_map/ppermute | solution.py:375
  145.6 14.7 %copy-start.8 = (bf16[2,128,1024]{2,1,0:T(8,128)(2,1)}, bf16[2,128,1024]{2,1,0:T(8,128)(2,1)S(1)}, u32[]{:S(2)}) copy-start(bf16[2,128,1024]{2,1,0:T(8,128)(2,1)S(1)} %add_add_fusion.3.refs_1_) | copy-start | bytes 1572868
  147.0 25.0 %collective-permute-start.43 = (bf16[256,1024]{1,0:T(8,128)(2,1)S(1)}, bf16[256,1024]{1,0:T(8,128)(2,1)S(1)}, u32[]{:S(2)}, u32[]{:S(2)}) collective-permute-start(bf16[256,1024]{1,0:T(8,128)(2,1)S(1)} %copy-done.15), channel_id=1, source_target_pairs={{0,1},{1,0},{2,3},{3,2},{4,5},{5,4},{6,7},{7,6},{8,9},{9,8},{10,11... | collective-permute-start | bytes 1572872 | tf_op jit(solution)/shard_map/ppermute | solution.py:345
  147.8 24.3 %collective-permute-start.18 = (bf16[2,128,1024]{2,1,0:T(8,128)(2,1)S(1)}, bf16[2,128,1024]{2,1,0:T(8,128)(2,1)S(1)}, u32[]{:S(2)}, u32[]{:S(2)}) collective-permute-start(bf16[2,128,1024]{2,1,0:T(8,128)(2,1)S(1)} %add_add_fusion.2.refs_1_), channel_id=1, source_target_pairs={{0,4},{4,0},{8,12},{12,8},{16,20},{20,16},{24,28},{28,24},{1,5},{5... | collective-permute-start | bytes 1572872 | tf_op jit(solution)/shard_map/ppermute | solution.py:375
  160.3 25.0 %collective-permute-start.4 = (bf16[2,128,1024]{2,1,0:T(8,128)(2,1)S(1)}, bf16[2,128,1024]{2,1,0:T(8,128)(2,1)S(1)}, u32[]{:S(2)}, u32[]{:S(2)}) collective-permute-start(bf16[2,128,1024]{2,1,0:T(8,128)(2,1)S(1)} %add_add_fusion.3.refs_1_), channel_id=1, source_target_pairs={{0,4},{4,0},{8,12},{12,8},{16,20},{20,16},{24,28},{28,24},{1,5},{5... | collective-permute-start | bytes 1572872 | tf_op jit(solution)/shard_map/ppermute | solution.py:375
  171.9 14.5 %collective-permute-start.35 = (bf16[4,32,1024]{2,1,0:T(8,128)(2,1)}, bf16[4,32,1024]{2,1,0:T(8,128)(2,1)S(1)}, u32[]{:S(2)}, u32[]{:S(2)}) collective-permute-start(bf16[4,32,1024]{2,1,0:T(8,128)(2,1)} %get-tuple-element.50), channel_id=1, source_target_pairs={{0,1},{1,0},{2,3},{3,2},{4,5},{5,4},{6,7},{7,6},{8,9},{9,8},{10,11... | collective-permute-start | bytes 786440 | tf_op jit(solution)/shard_map/ppermute | solution.py:345
  172.1 13.2 %copy-start.35 = (bf16[4,32,1024]{2,1,0:T(8,128)(2,1)S(1)}, bf16[4,32,1024]{2,1,0:T(8,128)(2,1)}, u32[]{:S(2)}) copy-start(bf16[4,32,1024]{2,1,0:T(8,128)(2,1)} %get-tuple-element.44) | copy-start | bytes 786436
  172.1 13.6 %copy-start.33 = (bf16[4,32,1024]{2,1,0:T(8,128)(2,1)S(1)}, bf16[4,32,1024]{2,1,0:T(8,128)(2,1)}, u32[]{:S(2)}) copy-start(bf16[4,32,1024]{2,1,0:T(8,128)(2,1)} %get-tuple-element.45) | copy-start | bytes 786436
  172.1 14.4 %copy-start.29 = (bf16[4,32,1024]{2,1,0:T(8,128)(2,1)S(1)}, bf16[4,32,1024]{2,1,0:T(8,128)(2,1)}, u32[]{:S(2)}) copy-start(bf16[4,32,1024]{2,1,0:T(8,128)(2,1)} %get-tuple-element.46) | copy-start | bytes 786436
  172.1 15.2 %collective-permute-start.36 = (bf16[4,32,1024]{2,1,0:T(8,128)(2,1)}, bf16[4,32,1024]{2,1,0:T(8,128)(2,1)S(1)}, u32[]{:S(2)}, u32[]{:S(2)}) collective-permute-start(bf16[4,32,1024]{2,1,0:T(8,128)(2,1)} %get-tuple-element.51), channel_id=1, source_target_pairs={{0,2},{1,3},{2,0},{3,1},{4,6},{5,7},{6,4},{7,5},{8,10},{9,11},{10,... | collective-permute-start | bytes 786440 | tf_op jit(solution)/shard_map/ppermute | solution.py:345
  184.2 14.8 %collective-permute-start.37 = (bf16[4,32,1024]{2,1,0:T(8,128)(2,1)S(1)}, bf16[4,32,1024]{2,1,0:T(8,128)(2,1)S(1)}, u32[]{:S(2)}, u32[]{:S(2)}) collective-permute-start(bf16[4,32,1024]{2,1,0:T(8,128)(2,1)S(1)} %copy-done.34), channel_id=1, source_target_pairs={{0,3},{1,2},{2,1},{3,0},{4,7},{5,6},{6,5},{7,4},{8,11},{9,10},{10,... | collective-permute-start | bytes 786440 | tf_op jit(solution)/shard_map/ppermute | solution.py:345
  185.3 14.6 %collective-permute-start.27 = (bf16[4,32,1024]{2,1,0:T(8,128)(2,1)S(1)}, bf16[4,32,1024]{2,1,0:T(8,128)(2,1)S(1)}, u32[]{:S(2)}, u32[]{:S(2)}) collective-permute-start(bf16[4,32,1024]{2,1,0:T(8,128)(2,1)S(1)} %copy-done.35), channel_id=1, source_target_pairs={{0,1},{1,0},{2,3},{3,2},{4,5},{5,4},{6,7},{7,6},{8,9},{9,8},{10,11... | collective-permute-start | bytes 786440 | tf_op jit(solution)/shard_map/ppermute | solution.py:345
  185.7 15.0 %collective-permute-start.28 = (bf16[4,32,1024]{2,1,0:T(8,128)(2,1)S(1)}, bf16[4,32,1024]{2,1,0:T(8,128)(2,1)S(1)}, u32[]{:S(2)}, u32[]{:S(2)}) collective-permute-start(bf16[4,32,1024]{2,1,0:T(8,128)(2,1)S(1)} %copy-done.33), channel_id=1, source_target_pairs={{0,2},{1,3},{2,0},{3,1},{4,6},{5,7},{6,4},{7,5},{8,10},{9,11},{10,... | collective-permute-start | bytes 786440 | tf_op jit(solution)/shard_map/ppermute | solution.py:345
  186.5 17.0 %collective-permute-start.29 = (bf16[4,32,1024]{2,1,0:T(8,128)(2,1)S(1)}, bf16[4,32,1024]{2,1,0:T(8,128)(2,1)S(1)}, u32[]{:S(2)}, u32[]{:S(2)}) collective-permute-start(bf16[4,32,1024]{2,1,0:T(8,128)(2,1)S(1)} %copy-done.29), channel_id=1, source_target_pairs={{0,3},{1,2},{2,1},{3,0},{4,7},{5,6},{6,5},{7,4},{8,11},{9,10},{10,... | collective-permute-start | bytes 786440 | tf_op jit(solution)/shard_map/ppermute | solution.py:345
  187.3 17.7 %collective-permute-start.19 = (bf16[4,32,1024]{2,1,0:T(8,128)(2,1)}, bf16[4,32,1024]{2,1,0:T(8,128)(2,1)S(1)}, u32[]{:S(2)}, u32[]{:S(2)}) collective-permute-start(bf16[4,32,1024]{2,1,0:T(8,128)(2,1)} %get-tuple-element.38), channel_id=1, source_target_pairs={{0,1},{1,0},{2,3},{3,2},{4,5},{5,4},{6,7},{7,6},{8,9},{9,8},{10,11... | collective-permute-start | bytes 786440 | tf_op jit(solution)/shard_map/ppermute | solution.py:345
  199.0 26.9 %copy-start.25 = (bf16[4,32,1024]{2,1,0:T(8,128)(2,1)}, bf16[4,32,1024]{2,1,0:T(8,128)(2,1)S(1)}, u32[]{:S(2)}) copy-start(bf16[4,32,1024]{2,1,0:T(8,128)(2,1)S(1)} %collective-permute-done.37.refs_16_) | copy-start | bytes 786436
  199.0 11.3 %collective-permute-start.20 = (bf16[4,32,1024]{2,1,0:T(8,128)(2,1)S(1)}, bf16[4,32,1024]{2,1,0:T(8,128)(2,1)S(1)}, u32[]{:S(2)}, u32[]{:S(2)}) collective-permute-start(bf16[4,32,1024]{2,1,0:T(8,128)(2,1)S(1)} %copy-done.31), channel_id=1, source_target_pairs={{0,2},{1,3},{2,0},{3,1},{4,6},{5,7},{6,4},{7,5},{8,10},{9,11},{10,... | collective-permute-start | bytes 786440 | tf_op jit(solution)/shard_map/ppermute | solution.py:345
  199.9 26.1 %copy-start.26 = (bf16[4,32,1024]{2,1,0:T(8,128)(2,1)}, bf16[4,32,1024]{2,1,0:T(8,128)(2,1)S(1)}, u32[]{:S(2)}) copy-start(bf16[4,32,1024]{2,1,0:T(8,128)(2,1)S(1)} %collective-permute-done.27.refs_10_) | copy-start | bytes 786436
  199.9 14.9 %collective-permute-start.21 = (bf16[4,32,1024]{2,1,0:T(8,128)(2,1)S(1)}, bf16[4,32,1024]{2,1,0:T(8,128)(2,1)S(1)}, u32[]{:S(2)}, u32[]{:S(2)}) collective-permute-start(bf16[4,32,1024]{2,1,0:T(8,128)(2,1)S(1)} %copy-done.30), channel_id=1, source_target_pairs={{0,3},{1,2},{2,1},{3,0},{4,7},{5,6},{6,5},{7,4},{8,11},{9,10},{10,... | collective-permute-start | bytes 786440 | tf_op jit(solution)/shard_map/ppermute | solution.py:345
  200.7 25.3 %copy-start.27 = (bf16[4,32,1024]{2,1,0:T(8,128)(2,1)}, bf16[4,32,1024]{2,1,0:T(8,128)(2,1)S(1)}, u32[]{:S(2)}) copy-start(bf16[4,32,1024]{2,1,0:T(8,128)(2,1)S(1)} %collective-permute-done.28.refs_11_) | copy-start | bytes 786436
  200.7 14.0 %collective-permute-start.11 = (bf16[4,32,1024]{2,1,0:T(8,128)(2,1)}, bf16[4,32,1024]{2,1,0:T(8,128)(2,1)S(1)}, u32[]{:S(2)}, u32[]{:S(2)}) collective-permute-start(bf16[4,32,1024]{2,1,0:T(8,128)(2,1)} %get-tuple-element.32), channel_id=1, source_target_pairs={{0,1},{1,0},{2,3},{3,2},{4,5},{5,4},{6,7},{7,6},{8,9},{9,8},{10,11... | collective-permute-start | bytes 786440 | tf_op jit(solution)/shard_map/ppermute | solution.py:345
  203.5 22.5 %copy-start.28 = (bf16[4,32,1024]{2,1,0:T(8,128)(2,1)}, bf16[4,32,1024]{2,1,0:T(8,128)(2,1)S(1)}, u32[]{:S(2)}) copy-start(bf16[4,32,1024]{2,1,0:T(8,128)(2,1)S(1)} %collective-permute-done.29.refs_12_) | copy-start | bytes 786436
  203.5 18.0 %collective-permute-start.12 = (bf16[4,32,1024]{2,1,0:T(8,128)(2,1)}, bf16[4,32,1024]{2,1,0:T(8,128)(2,1)S(1)}, u32[]{:S(2)}, u32[]{:S(2)}) collective-permute-start(bf16[4,32,1024]{2,1,0:T(8,128)(2,1)} %get-tuple-element.33), channel_id=1, source_target_pairs={{0,2},{1,3},{2,0},{3,1},{4,6},{5,7},{6,4},{7,5},{8,10},{9,11},{10,... | collective-permute-start | bytes 786440 | tf_op jit(solution)/shard_map/ppermute | solution.py:345
  205.0 21.0 %copy-start.32 = (bf16[4,32,1024]{2,1,0:T(8,128)(2,1)}, bf16[4,32,1024]{2,1,0:T(8,128)(2,1)S(1)}, u32[]{:S(2)}) copy-start(bf16[4,32,1024]{2,1,0:T(8,128)(2,1)S(1)} %collective-permute-done.19.refs_6_) | copy-start | bytes 786436
  205.0 21.0 %collective-permute-start.13 = (bf16[4,32,1024]{2,1,0:T(8,128)(2,1)}, bf16[4,32,1024]{2,1,0:T(8,128)(2,1)S(1)}, u32[]{:S(2)}, u32[]{:S(2)}) collective-permute-start(bf16[4,32,1024]{2,1,0:T(8,128)(2,1)} %get-tuple-element.34), channel_id=1, source_target_pairs={{0,3},{1,2},{2,1},{3,0},{4,7},{5,6},{6,5},{7,4},{8,11},{9,10},{10,... | collective-permute-start | bytes 786440 | tf_op jit(solution)/shard_map/ppermute | solution.py:345
  210.3 15.7 %copy-start.36 = (bf16[4,32,1024]{2,1,0:T(8,128)(2,1)}, bf16[4,32,1024]{2,1,0:T(8,128)(2,1)S(1)}, u32[]{:S(2)}) copy-start(bf16[4,32,1024]{2,1,0:T(8,128)(2,1)S(1)} %collective-permute-done.20.refs_7_) | copy-start | bytes 786436
  (21 other events, 151.7 us)

commit v2 on v1

--- a/solution.py
+++ b/solution.py
@@ -174,7 +174,7 @@
             pltpu.VMEM((3, tokens, 2 * channels // HEADS), BF16),
             *weight_scratch(channels, n_space),
         ],
-        compiler_params=pltpu.CompilerParams(vmem_limit_bytes=60 << 20),
+        compiler_params=pltpu.CompilerParams(vmem_limit_bytes=28 << 20),
         cost_estimate=pl.CostEstimate(
             flops=tokens * channels * (8 * channels + 4 * width),
             bytes_accessed=4 * tokens * channels + 8 * channels * channels,
@@ -282,7 +282,7 @@
             pltpu.VMEM((3, tokens, 2 * channels // HEADS), BF16),
             *weight_scratch(channels, n_space),
         ],
-        compiler_params=pltpu.CompilerParams(vmem_limit_bytes=60 << 20),
+        compiler_params=pltpu.CompilerParams(vmem_limit_bytes=48 << 20),
         cost_estimate=pl.CostEstimate(
             flops=rows * cols * channels * (8 * channels + 4 * rows),
             bytes_accessed=4 * rows * cols * channels + 8 * channels * channels,
@@ -325,9 +325,11 @@
     def own_half(i, which):
         return lax.dynamic_slice_in_dim(slab, (2 * i + which) * half, half, 0) * owned
 
+    first, owned = lax.optimization_barrier((own_half(0, 1 - side), owned))
     sends, keeps = lax.optimization_barrier(
-        ([own_half(i, 1 - side) for i in range(chunks)], [own_half(i, side) for i in range(chunks)])
+        ([own_half(i, 1 - side) for i in range(1, chunks)], [own_half(i, side) for i in range(chunks)])
     )
+    sends = [first] + sends
     swap = [(l, l ^ 1) for l in range(n_lead)]
     hops = [
         [

time: 264 us -> 259 us (0.981)
  Pallas kernels: 80.8 us -> 70.1 us
  waiting for transfers between devices: 117 us -> 122 us
    pallas_call x4, Pallas kernels: 44.2 us -> 35.6 us  [row_call(): pl.pallas_call(lambda *refs: row_kernel(n_space, *refs), out_shape=[jax.S...]
    ppermute x24, waiting for transfers between devices: 29.3 us -> 32.5 us  [across(): return lax.ppermute(value, 'space', [(s, s ^ j) for s in range(n_space)])]
  transfers between devices with their start and end apart: 44 -> 44, of which waited for: 17 -> 20; matrix products, arithmetic and copies ran while one was open for 3% -> 3% of each run, Pallas kernels for 17% -> 14%
where the time goes in v2:
time: 259 us; the launch traced here: 258 us
  waiting for transfers between devices  122 us (47%)
  Pallas kernels  70.1 us (27%)
  starting transfers between devices  48.1 us (19%)
  other arithmetic  14.6 us (6%)
    ppermute x12, waiting for transfers between devices, on_device(): terms.append(lax.ppermute(send, 'lead', pairs))  56.9 us
    pallas_call x4, Pallas kernels, row_call(): pl.pallas_call(lambda *refs: row_kernel(n_space, *refs), out_shape=[jax.S...  35.6 us
    pallas_call x1, Pallas kernels, col_call(): pl.pallas_call(lambda *refs: col_kernel(n_chunks, n_space, *refs), out_sh...  34.5 us
    ppermute x24, waiting for transfers between devices, across(): return lax.ppermute(value, 'space', [(s, s ^ j) for s in range(n_space)])  32.5 us
    ppermute x4, waiting for transfers between devices, on_device(): got = lax.ppermute(sends[i], 'lead', swap)  29.2 us
    ppermute x12, starting transfers between devices, on_device(): terms.append(lax.ppermute(send, 'lead', pairs))  20.8 us
    ppermute x24, starting transfers between devices, across(): return lax.ppermute(value, 'space', [(s, s ^ j) for s in range(n_space)])  14.2 us
    ppermute x4, starting transfers between devices, on_device(): got = lax.ppermute(sends[i], 'lead', swap)  7.08 us
  transfers between devices with their start and end apart: 44, of which 20 were waited for; matrix products, arithmetic and copies ran while one was open for 3% of the time, Pallas kernels for 14%

profile of v2, /device:TPU:0, one launch (start us, length us, event | category | flops | bytes accessed | tf_op | source)
XLA Modules:
  0.0 258.2 jit_solution(15793428908200556870)
XLA Ops:
  0.0 1.3 fusion
  1.3 1.7 multiply_bitcast_fusion.7
  3.0 3.0 %multiply_bitcast_fusion = (bf16[2,128,1024]{2,1,0:T(8,128)(2,1)S(1)}, bf16[2,128,1024]{2,1,0:T(8,128)(2,1)S(1)}, bf16[2,128,1024]{2,1,0:T(8,128)(2,1)S(1)}, bf1...) fusion(bf16[1,16,128,1024]{3,2,1,0:T(8,128)(2,1)} %param.10, ...), kind=kLoop, calls=%fused_computation.4 | loop fusion | flops 1835008 | bytes 7340062 | tf_op jit(solution)/shard_map/mul | solution.py:326
  6.0 3.0 %collective-permute-start.30 = (bf16[2,128,1024]{2,1,0:T(8,128)(2,1)S(1)}, bf16[2,128,1024]{2,1,0:T(8,128)(2,1)S(1)}, u32[]{:S(2)}, u32[]{:S(2)}) collective-permute-start(bf16[2,128,1024]{2,1,0:T(8,128)(2,1)S(1)} %get-tuple-element.50), channel_id=1, source_target_pairs={{0,4},{4,0},{8,12},{12,8},{16,20},{20,16},{24,28},{28,24},{1,5},{5... | collective-permute-start | bytes 1572872 | tf_op jit(solution)/shard_map/ppermute | solution.py:368
  9.0 1.5 collective-permute-start.8
  11.1 1.5 collective-permute-start.14
  12.6 9.2 %collective-permute-done.30 = bf16[2,128,1024]{2,1,0:T(8,128)(2,1)S(1)} collective-permute-done((bf16[2,128,1024]{2,1,0:T(8,128)(2,1)S(1)}, bf16[2,128,1024]{2,1,0:T(8,128)(2,1)S(1)}, u32[]{:S(2)}, u32[]{:S(2)}) %collective-permute-start.30) | collective-permute-done | bytes 524320 | tf_op jit(solution)/shard_map/ppermute | solution.py:368
  21.8 2.0 collective-permute-start
  23.8 1.6 collective-permute-start.41
  25.6 7.4 %collective-permute-done.22 = bf16[2,128,1024]{2,1,0:T(8,128)(2,1)S(1)} collective-permute-done((bf16[2,128,1024]{2,1,0:T(8,128)(2,1)S(1)}, bf16[2,128,1024]{2,1,0:T(8,128)(2,1)S(1)}, u32[]{:S(2)}, u32[]{:S(2)}) %collective-permute-start.22) | collective-permute-done | bytes 524320 | tf_op jit(solution)/shard_map/ppermute | solution.py:368
  33.0 4.0 %collective-permute-start.31 = (bf16[2,128,1024]{2,1,0:T(8,128)(2,1)S(1)}, bf16[2,128,1024]{2,1,0:T(8,128)(2,1)S(1)}, u32[]{:S(2)}, u32[]{:S(2)}) collective-permute-start(bf16[2,128,1024]{2,1,0:T(8,128)(2,1)S(1)} %add.156), channel_id=1, source_target_pairs={{24,16},{0,8},{28,20},{4,12},{25,17},{1,9},{29,21},{5,13},{26,18},... | collective-permute-start | bytes 1572872 | tf_op jit(solution)/shard_map/ppermute | solution.py:373
  37.3 0.8 copy-done.11
  38.1 6.2 %collective-permute-done.14 = bf16[2,128,1024]{2,1,0:T(8,128)(2,1)S(1)} collective-permute-done((bf16[2,128,1024]{2,1,0:T(8,128)(2,1)S(1)}, bf16[2,128,1024]{2,1,0:T(8,128)(2,1)S(1)}, u32[]{:S(2)}, u32[]{:S(2)}) %collective-permute-start.14) | collective-permute-done | bytes 524320 | tf_op jit(solution)/shard_map/ppermute | solution.py:368
  44.3 4.0 %collective-permute-start.23 = (bf16[2,128,1024]{2,1,0:T(8,128)(2,1)S(1)}, bf16[2,128,1024]{2,1,0:T(8,128)(2,1)S(1)}, u32[]{:S(2)}, u32[]{:S(2)}) collective-permute-start(bf16[2,128,1024]{2,1,0:T(8,128)(2,1)S(1)} %add.151), channel_id=1, source_target_pairs={{24,16},{0,8},{28,20},{4,12},{25,17},{1,9},{29,21},{5,13},{26,18},... | collective-permute-start | bytes 1572872 | tf_op jit(solution)/shard_map/ppermute | solution.py:373
  48.3 6.3 %collective-permute-done = bf16[2,128,1024]{2,1,0:T(8,128)(2,1)S(1)} collective-permute-done((bf16[2,128,1024]{2,1,0:T(8,128)(2,1)S(1)}, bf16[2,128,1024]{2,1,0:T(8,128)(2,1)S(1)}, u32[]{:S(2)}, u32[]{:S(2)}) %collective-permute-start) | collective-permute-done | bytes 524320 | tf_op jit(solution)/shard_map/ppermute | solution.py:368
  54.7 1.8 collective-permute-start.7
  56.7 3.5 %collective-permute-start.15 = (bf16[2,128,1024]{2,1,0:T(8,128)(2,1)S(1)}, bf16[2,128,1024]{2,1,0:T(8,128)(2,1)S(1)}, u32[]{:S(2)}, u32[]{:S(2)}) collective-permute-start(bf16[2,128,1024]{2,1,0:T(8,128)(2,1)S(1)} %add.146), channel_id=1, source_target_pairs={{24,16},{0,8},{28,20},{4,12},{25,17},{1,9},{29,21},{5,13},{26,18},... | collective-permute-start | bytes 1572872 | tf_op jit(solution)/shard_map/ppermute | solution.py:373
  60.7 1.3 collective-permute-start.1
  62.1 0.7 collective-permute-start.32
  63.0 9.5 %collective-permute-done.15 = bf16[2,128,1024]{2,1,0:T(8,128)(2,1)S(1)} collective-permute-done((bf16[2,128,1024]{2,1,0:T(8,128)(2,1)S(1)}, bf16[2,128,1024]{2,1,0:T(8,128)(2,1)S(1)}, u32[]{:S(2)}, u32[]{:S(2)}) %collective-permute-start.15) | collective-permute-done | bytes 524320 | tf_op jit(solution)/shard_map/ppermute | solution.py:373
  72.5 0.7 collective-permute-start.24
  73.4 0.7 collective-permute-start.16
  74.1 7.3 %collective-permute-done.1 = bf16[2,128,1024]{2,1,0:T(8,128)(2,1)S(1)} collective-permute-done((bf16[2,128,1024]{2,1,0:T(8,128)(2,1)S(1)}, bf16[2,128,1024]{2,1,0:T(8,128)(2,1)S(1)}, u32[]{:S(2)}, u32[]{:S(2)}) %collective-permute-start.1) | collective-permute-done | bytes 524320 | tf_op jit(solution)/shard_map/ppermute | solution.py:373
  82.2 0.7 collective-permute-start.2
  82.9 1.0 add.159
  84.0 1.3 collective-permute-start.33
  85.3 6.7 %collective-permute-done.7.refs_9_ = bf16[256,3072]{1,0:T(8,128)(2,1)S(1)} collective-permute-done((bf16[256,3072]{1,0:T(8,128)(2,1)S(1)}, bf16[256,3072]{1,0:T(8,128)(2,1)S(1)}, u32[]{:S(2)}, u32[]{:S(2)}) %collective-permute-start.7) | collective-permute-done | bytes 1572896 | tf_op jit(solution)/shard_map/ppermute | solution.py:347
  91.9 1.0 add.154
  93.0 0.8 copy-done.29
  93.8 1.3 collective-permute-start.25
  95.8 0.9 dynamic-slice_add_fusion
  96.7 1.5 add.149
  98.4 13.2 %collective-permute-done.33 = bf16[2,128,1024]{2,1,0:T(8,128)(2,1)} collective-permute-done((bf16[2,128,1024]{2,1,0:T(8,128)(2,1)}, bf16[2,128,1024]{2,1,0:T(8,128)(2,1)}, u32[]{:S(2)}, u32[]{:S(2)}) %collective-permute-start.33) | collective-permute-done | bytes 524320 | tf_op jit(solution)/shard_map/ppermute | solution.py:373
  111.6 1.3 collective-permute-start.17
  112.9 1.1 add_add_fusion.refs_1_
  114.0 12.4 %collective-permute-done.25 = bf16[2,128,1024]{2,1,0:T(8,128)(2,1)} collective-permute-done((bf16[2,128,1024]{2,1,0:T(8,128)(2,1)}, bf16[2,128,1024]{2,1,0:T(8,128)(2,1)}, u32[]{:S(2)}, u32[]{:S(2)}) %collective-permute-start.25) | collective-permute-done | bytes 524320 | tf_op jit(solution)/shard_map/ppermute | solution.py:373
  126.5 1.3 collective-permute-start.3
  127.8 1.1 add_add_fusion.1.refs_1_
  129.5 8.1 %collective-permute-done.17 = bf16[2,128,1024]{2,1,0:T(8,128)(2,1)S(1)} collective-permute-done((bf16[2,128,1024]{2,1,0:T(8,128)(2,1)S(1)}, bf16[2,128,1024]{2,1,0:T(8,128)(2,1)S(1)}, u32[]{:S(2)}, u32[]{:S(2)}) %collective-permute-start.17) | collective-permute-done | bytes 524320 | tf_op jit(solution)/shard_map/ppermute | solution.py:373
  137.6 1.5 collective-permute-start.34
  139.3 6.4 %collective-permute-done.3 = bf16[2,128,1024]{2,1,0:T(8,128)(2,1)S(1)} collective-permute-done((bf16[2,128,1024]{2,1,0:T(8,128)(2,1)S(1)}, bf16[2,128,1024]{2,1,0:T(8,128)(2,1)S(1)}, u32[]{:S(2)}, u32[]{:S(2)}) %collective-permute-start.3) | collective-permute-done | bytes 524320 | tf_op jit(solution)/shard_map/ppermute | solution.py:373
  145.6 1.5 collective-permute-start.26
  147.2 1.3 collective-permute-done.34.refs_2_
  148.5 1.6 collective-permute-start.18
  150.1 9.0 %row_attention.7 = (bf16[4,32,1024]{2,1,0:T(8,128)(2,1)S(1)}, bf16[4,32,1024]{2,1,0:T(8,128)(2,1)S(1)}, bf16[4,32,1024]{2,1,0:T(8,128)(2,1)S(1)}, bf16[4,32,1024]{2,1,0:T(8,128)(2,1)S(1)}) custom-call(s32[2]{0:T(128)S(1)} %pad_add_fusion.refs_0_, bf16[2,128,1024]{2,1,0:T(8,128)(2,1)S(1)} %add_add_fusion.refs_1_, ...), custom_call_target="tpu_custom_call" | custom-call | flops 4563402752 | bytes 10485760 | tf_op jit(solution)/shard_map/row_attention/pallas_call | solution.py:163
  159.1 1.3 collective-permute-done.26.refs_2_
  160.4 1.5 collective-permute-start.4
  161.9 8.8 %row_attention.6 = (bf16[4,32,1024]{2,1,0:T(8,128)(2,1)S(1)}, bf16[4,32,1024]{2,1,0:T(8,128)(2,1)S(1)}, bf16[4,32,1024]{2,1,0:T(8,128)(2,1)S(1)}, bf16[4,32,1024]{2,1,0:T(8,128)(2,1)S(1)}) custom-call(s32[2]{0:T(128)S(1)} %pad_add_fusion.refs_0_, bf16[2,128,1024]{2,1,0:T(8,128)(2,1)S(1)} %add_add_fusion.1.refs_1_, ...), custom_call_target="tpu_custom_call" | custom-call | flops 4563402752 | bytes 10485760 | tf_op jit(solution)/shard_map/row_attention/pallas_call | solution.py:163
  170.8 0.8 collective-permute-done.18.refs_2_
  172.2 9.0 %row_attention.5 = (bf16[4,32,1024]{2,1,0:T(8,128)(2,1)S(1)}, bf16[4,32,1024]{2,1,0:T(8,128)(2,1)S(1)}, bf16[4,32,1024]{2,1,0:T(8,128)(2,1)S(1)}, bf16[4,32,1024]{2,1,0:T(8,128)(2,1)S(1)}) custom-call(s32[2]{0:T(128)S(1)} %pad_add_fusion.refs_0_, bf16[2,128,1024]{2,1,0:T(8,128)(2,1)S(1)} %add_add_fusion.2.refs_1_, ...), custom_call_target="tpu_custom_call" | custom-call | flops 4563402752 | bytes 10485760 | tf_op jit(solution)/shard_map/row_attention/pallas_call | solution.py:163
  181.2 0.6 collective-permute-start.37
  181.8 1.1 collective-permute-start.27
  183.4 0.9 collective-permute-start.29
  184.4 0.8 collective-permute-start.19
  185.2 8.8 %row_attention.4 = (bf16[4,32,1024]{2,1,0:T(8,128)(2,1)S(1)}, bf16[4,32,1024]{2,1,0:T(8,128)(2,1)S(1)}, bf16[4,32,1024]{2,1,0:T(8,128)(2,1)S(1)}, bf16[4,32,1024]{2,1,0:T(8,128)(2,1)S(1)}) custom-call(s32[2]{0:T(128)S(1)} %pad_add_fusion.refs_0_, bf16[2,128,1024]{2,1,0:T(8,128)(2,1)S(1)} %add_add_fusion.3.refs_1_, ...), custom_call_target="tpu_custom_call" | custom-call | flops 4563402752 | bytes 10485760 | tf_op jit(solution)/shard_map/row_attention/pallas_call | solution.py:163
  194.6 0.9 collective-permute-start.21
  195.6 0.6 collective-permute-start.11
  196.2 4.8 %collective-permute-done.29.refs_12_ = bf16[4,32,1024]{2,1,0:T(8,128)(2,1)S(1)} collective-permute-done((bf16[4,32,1024]{2,1,0:T(8,128)(2,1)S(1)}, bf16[4,32,1024]{2,1,0:T(8,128)(2,1)S(1)}, u32[]{:S(2)}, u32[]{:S(2)}) %collective-permute-start.29) | collective-permute-done | bytes 262176 | tf_op jit(solution)/shard_map/ppermute | solution.py:347
  201.1 1.6 collective-permute-start.12
  202.7 4.2 %collective-permute-done.20.refs_7_ = bf16[4,32,1024]{2,1,0:T(8,128)(2,1)S(1)} collective-permute-done((bf16[4,32,1024]{2,1,0:T(8,128)(2,1)S(1)}, bf16[4,32,1024]{2,1,0:T(8,128)(2,1)S(1)}, u32[]{:S(2)}, u32[]{:S(2)}) %collective-permute-start.20) | collective-permute-done | bytes 262176 | tf_op jit(solution)/shard_map/ppermute | solution.py:347
  206.8 5.5 %collective-permute-done.21.refs_8_ = bf16[4,32,1024]{2,1,0:T(8,128)(2,1)S(1)} collective-permute-done((bf16[4,32,1024]{2,1,0:T(8,128)(2,1)S(1)}, bf16[4,32,1024]{2,1,0:T(8,128)(2,1)S(1)}, u32[]{:S(2)}, u32[]{:S(2)}) %collective-permute-start.21) | collective-permute-done | bytes 262176 | tf_op jit(solution)/shard_map/ppermute | solution.py:347
  212.3 5.8 %collective-permute-done.12.refs_3_ = bf16[4,32,1024]{2,1,0:T(8,128)(2,1)S(1)} collective-permute-done((bf16[4,32,1024]{2,1,0:T(8,128)(2,1)S(1)}, bf16[4,32,1024]{2,1,0:T(8,128)(2,1)S(1)}, u32[]{:S(2)}, u32[]{:S(2)}) %collective-permute-start.12) | collective-permute-done | bytes 262176 | tf_op jit(solution)/shard_map/ppermute | solution.py:347
  218.1 5.5 %collective-permute-done.13.refs_4_ = bf16[4,32,1024]{2,1,0:T(8,128)(2,1)S(1)} collective-permute-done((bf16[4,32,1024]{2,1,0:T(8,128)(2,1)S(1)}, bf16[4,32,1024]{2,1,0:T(8,128)(2,1)S(1)}, u32[]{:S(2)}, u32[]{:S(2)}) %collective-permute-start.13) | collective-permute-done | bytes 262176 | tf_op jit(solution)/shard_map/ppermute | solution.py:347
  223.5 34.5 %col_attention.1 = bf16[64,32,1024]{2,1,0:T(8,128)(2,1)} custom-call(s32[2]{0:T(128)S(1)} %pad_add_fusion.refs_0_, bf16[4,32,1024]{2,1,0:T(8,128)(2,1)S(1)} %get-tuple-element.33.refs_1_, bf16[4,32,1024]{2,1,0:T(8,128)(2,1)S(1)} %collective-permute-done.11.refs_2_, bf16[4,32,1024]{2,1,0:T(8,128)(2,1)S(1)} %collective-permute-done.12.refs_3_, ...), custom_call_target="tpu_custom_call" | custom-call | flops 17716740096 | bytes 16777216 | tf_op jit(solution)/shard_map/col_attention/pallas_call | solution.py:270
  (126 shorter events, 5.7 us)
Async XLA Ops:
  3.0 20.8 %copy-start.3 = (bf16[256,1024]{1,0:T(8,128)(2,1)S(1)}, bf16[256,1024]{1,0:T(8,128)(2,1)}, u32[]{:S(2)}) copy-start(bf16[256,1024]{1,0:T(8,128)(2,1)} %refs_19_.1) | copy-start | bytes 1572868
  6.0 48.7 %copy-start = (bf16[256,3072]{1,0:T(8,128)(2,1)S(1)}, bf16[256,3072]{1,0:T(8,128)(2,1)}, u32[]{:S(2)}) copy-start(bf16[256,3072]{1,0:T(8,128)(2,1)} %refs_5_.7) | copy-start | bytes 4718596
  6.0 15.8 %collective-permute-start.30 = (bf16[2,128,1024]{2,1,0:T(8,128)(2,1)S(1)}, bf16[2,128,1024]{2,1,0:T(8,128)(2,1)S(1)}, u32[]{:S(2)}, u32[]{:S(2)}) collective-permute-start(bf16[2,128,1024]{2,1,0:T(8,128)(2,1)S(1)} %get-tuple-element.50), channel_id=1, source_target_pairs={{0,4},{4,0},{8,12},{12,8},{16,20},{20,16},{24,28},{28,24},{1,5},{5... | collective-permute-start | bytes 1572872 | tf_op jit(solution)/shard_map/ppermute | solution.py:368
  9.0 14.8 %collective-permute-start.8 = (bf16[256,1024]{1,0:T(8,128)(2,1)S(1)}, bf16[256,1024]{1,0:T(8,128)(2,1)S(1)}, u32[]{:S(2)}, u32[]{:S(2)}) collective-permute-start(bf16[256,1024]{1,0:T(8,128)(2,1)S(1)} %copy-done.1), channel_id=1, source_target_pairs={{0,2},{1,3},{2,0},{3,1},{4,6},{5,7},{6,4},{7,5},{8,10},{9,11},{10,... | collective-permute-start | bytes 1572872 | tf_op jit(solution)/shard_map/ppermute | solution.py:347
  10.6 22.5 %collective-permute-start.22 = (bf16[2,128,1024]{2,1,0:T(8,128)(2,1)S(1)}, bf16[2,128,1024]{2,1,0:T(8,128)(2,1)S(1)}, u32[]{:S(2)}, u32[]{:S(2)}) collective-permute-start(bf16[2,128,1024]{2,1,0:T(8,128)(2,1)S(1)} %get-tuple-element.44), channel_id=1, source_target_pairs={{0,4},{4,0},{8,12},{12,8},{16,20},{20,16},{24,28},{28,24},{1,5},{5... | collective-permute-start | bytes 1572872 | tf_op jit(solution)/shard_map/ppermute | solution.py:368
  11.1 26.2 %collective-permute-start.6 = (bf16[256,1024]{1,0:T(8,128)(2,1)S(1)}, bf16[256,1024]{1,0:T(8,128)(2,1)S(1)}, u32[]{:S(2)}, u32[]{:S(2)}) collective-permute-start(bf16[256,1024]{1,0:T(8,128)(2,1)S(1)} %copy-done.1), channel_id=1, source_target_pairs={{0,1},{1,0},{2,3},{3,2},{4,5},{5,4},{6,7},{7,6},{8,9},{9,8},{10,11... | collective-permute-start | bytes 1572872 | tf_op jit(solution)/shard_map/ppermute | solution.py:347
  11.1 33.2 %collective-permute-start.14 = (bf16[2,128,1024]{2,1,0:T(8,128)(2,1)S(1)}, bf16[2,128,1024]{2,1,0:T(8,128)(2,1)S(1)}, u32[]{:S(2)}, u32[]{:S(2)}) collective-permute-start(bf16[2,128,1024]{2,1,0:T(8,128)(2,1)S(1)} %get-tuple-element.38), channel_id=1, source_target_pairs={{0,4},{4,0},{8,12},{12,8},{16,20},{20,16},{24,28},{28,24},{1,5},{5... | collective-permute-start | bytes 1572872 | tf_op jit(solution)/shard_map/ppermute | solution.py:368
  21.8 32.9 %collective-permute-start = (bf16[2,128,1024]{2,1,0:T(8,128)(2,1)S(1)}, bf16[2,128,1024]{2,1,0:T(8,128)(2,1)S(1)}, u32[]{:S(2)}, u32[]{:S(2)}) collective-permute-start(bf16[2,128,1024]{2,1,0:T(8,128)(2,1)S(1)} %multiply_bitcast_fusion.7), channel_id=1, source_target_pairs={{0,4},{4,0},{8,12},{12,8},{16,20},{20,16},{24,28},{28,24},{1,5},{5... | collective-permute-start | bytes 1572872 | tf_op jit(solution)/shard_map/ppermute | solution.py:368
  23.8 36.4 %copy-start.9 = (bf16[256,1024]{1,0:T(8,128)(2,1)}, bf16[256,1024]{1,0:T(8,128)(2,1)S(1)}, u32[]{:S(2)}) copy-start(bf16[256,1024]{1,0:T(8,128)(2,1)S(1)} %collective-permute-done.8.refs_10_) | copy-start | bytes 1572868
  23.8 32.8 %collective-permute-start.41 = (bf16[256,1024]{1,0:T(8,128)(2,1)S(1)}, bf16[256,1024]{1,0:T(8,128)(2,1)S(1)}, u32[]{:S(2)}, u32[]{:S(2)}) collective-permute-start(bf16[256,1024]{1,0:T(8,128)(2,1)S(1)} %copy-done.3), channel_id=1, source_target_pairs={{0,2},{1,3},{2,0},{3,1},{4,6},{5,7},{6,4},{7,5},{8,10},{9,11},{10,... | collective-permute-start | bytes 1572872 | tf_op jit(solution)/shard_map/ppermute | solution.py:347
  33.0 27.1 %collective-permute-start.31 = (bf16[2,128,1024]{2,1,0:T(8,128)(2,1)S(1)}, bf16[2,128,1024]{2,1,0:T(8,128)(2,1)S(1)}, u32[]{:S(2)}, u32[]{:S(2)}) collective-permute-start(bf16[2,128,1024]{2,1,0:T(8,128)(2,1)S(1)} %add.156), channel_id=1, source_target_pairs={{24,16},{0,8},{28,20},{4,12},{25,17},{1,9},{29,21},{5,13},{26,18},... | collective-permute-start | bytes 1572872 | tf_op jit(solution)/shard_map/ppermute | solution.py:373
  38.1 22.6 %collective-permute-start.39 = (bf16[256,1024]{1,0:T(8,128)(2,1)S(1)}, bf16[256,1024]{1,0:T(8,128)(2,1)S(1)}, u32[]{:S(2)}, u32[]{:S(2)}) collective-permute-start(bf16[256,1024]{1,0:T(8,128)(2,1)S(1)} %copy-done.3), channel_id=1, source_target_pairs={{0,1},{1,0},{2,3},{3,2},{4,5},{5,4},{6,7},{7,6},{8,9},{9,8},{10,11... | collective-permute-start | bytes 1572872 | tf_op jit(solution)/shard_map/ppermute | solution.py:347
  44.3 17.8 %collective-permute-start.23 = (bf16[2,128,1024]{2,1,0:T(8,128)(2,1)S(1)}, bf16[2,128,1024]{2,1,0:T(8,128)(2,1)S(1)}, u32[]{:S(2)}, u32[]{:S(2)}) collective-permute-start(bf16[2,128,1024]{2,1,0:T(8,128)(2,1)S(1)} %add.151), channel_id=1, source_target_pairs={{24,16},{0,8},{28,20},{4,12},{25,17},{1,9},{29,21},{5,13},{26,18},... | collective-permute-start | bytes 1572872 | tf_op jit(solution)/shard_map/ppermute | solution.py:373
  54.7 37.3 %collective-permute-start.7 = (bf16[256,3072]{1,0:T(8,128)(2,1)S(1)}, bf16[256,3072]{1,0:T(8,128)(2,1)S(1)}, u32[]{:S(2)}, u32[]{:S(2)}) collective-permute-start(bf16[256,3072]{1,0:T(8,128)(2,1)S(1)} %copy-done), channel_id=1, source_target_pairs={{0,2},{1,3},{2,0},{3,1},{4,6},{5,7},{6,4},{7,5},{8,10},{9,11},{10,... | collective-permute-start | bytes 4718600 | tf_op jit(solution)/shard_map/ppermute | solution.py:347
  56.6 16.5 %copy-start.16 = (bf16[2,128,1024]{2,1,0:T(8,128)(2,1)}, bf16[2,128,1024]{2,1,0:T(8,128)(2,1)S(1)}, u32[]{:S(2)}) copy-start(bf16[2,128,1024]{2,1,0:T(8,128)(2,1)S(1)} %add.146) | copy-start | bytes 1572868
  56.7 15.8 %collective-permute-start.15 = (bf16[2,128,1024]{2,1,0:T(8,128)(2,1)S(1)}, bf16[2,128,1024]{2,1,0:T(8,128)(2,1)S(1)}, u32[]{:S(2)}, u32[]{:S(2)}) collective-permute-start(bf16[2,128,1024]{2,1,0:T(8,128)(2,1)S(1)} %add.146), channel_id=1, source_target_pairs={{24,16},{0,8},{28,20},{4,12},{25,17},{1,9},{29,21},{5,13},{26,18},... | collective-permute-start | bytes 1572872 | tf_op jit(solution)/shard_map/ppermute | solution.py:373
  60.2 13.2 %collective-permute-start.10 = (bf16[256,1024]{1,0:T(8,128)(2,1)S(1)}, bf16[256,1024]{1,0:T(8,128)(2,1)S(1)}, u32[]{:S(2)}, u32[]{:S(2)}) collective-permute-start(bf16[256,1024]{1,0:T(8,128)(2,1)S(1)} %collective-permute-done.8.refs_10_), channel_id=1, source_target_pairs={{0,1},{1,0},{2,3},{3,2},{4,5},{5,4},{6,7},{7,6},{8,9},{9,8},{10,11... | collective-permute-start | bytes 1572872 | tf_op jit(solution)/shard_map/ppermute | solution.py:347
  60.5 21.5 %copy-start.17 = (bf16[2,128,1024]{2,1,0:T(8,128)(2,1)}, bf16[2,128,1024]{2,1,0:T(8,128)(2,1)S(1)}, u32[]{:S(2)}) copy-start(bf16[2,128,1024]{2,1,0:T(8,128)(2,1)S(1)} %add.138) | copy-start | bytes 1572868
  60.7 12.6 %copy-start.25 = (bf16[2,128,1024]{2,1,0:T(8,128)(2,1)}, bf16[2,128,1024]{2,1,0:T(8,128)(2,1)S(1)}, u32[]{:S(2)}) copy-start(bf16[2,128,1024]{2,1,0:T(8,128)(2,1)S(1)} %add.157) | copy-start | bytes 1572868
  60.7 12.6 %copy-start.7 = (bf16[256,1024]{1,0:T(8,128)(2,1)}, bf16[256,1024]{1,0:T(8,128)(2,1)S(1)}, u32[]{:S(2)}) copy-start(bf16[256,1024]{1,0:T(8,128)(2,1)S(1)} %collective-permute-done.39.refs_21_) | copy-start | bytes 1572868
  60.7 20.7 %collective-permute-start.1 = (bf16[2,128,1024]{2,1,0:T(8,128)(2,1)S(1)}, bf16[2,128,1024]{2,1,0:T(8,128)(2,1)S(1)}, u32[]{:S(2)}, u32[]{:S(2)}) collective-permute-start(bf16[2,128,1024]{2,1,0:T(8,128)(2,1)S(1)} %add.138), channel_id=1, source_target_pairs={{24,16},{0,8},{28,20},{4,12},{25,17},{1,9},{29,21},{5,13},{26,18},... | collective-permute-start | bytes 1572872 | tf_op jit(solution)/shard_map/ppermute | solution.py:373
  62.1 19.3 %collective-permute-start.32 = (bf16[2,128,1024]{2,1,0:T(8,128)(2,1)S(1)}, bf16[2,128,1024]{2,1,0:T(8,128)(2,1)S(1)}, u32[]{:S(2)}, u32[]{:S(2)}) collective-permute-start(bf16[2,128,1024]{2,1,0:T(8,128)(2,1)S(1)} %add.157), channel_id=1, source_target_pairs={{16,8},{8,16},{20,12},{12,20},{17,9},{9,17},{21,13},{13,21},{18,10... | collective-permute-start | bytes 1572872 | tf_op jit(solution)/shard_map/ppermute | solution.py:373
  63.0 19.2 %copy-start.27 = (bf16[2,128,1024]{2,1,0:T(8,128)(2,1)}, bf16[2,128,1024]{2,1,0:T(8,128)(2,1)S(1)}, u32[]{:S(2)}) copy-start(bf16[2,128,1024]{2,1,0:T(8,128)(2,1)S(1)} %add.152) | copy-start | bytes 1572868
  72.5 9.8 %collective-permute-start.24 = (bf16[2,128,1024]{2,1,0:T(8,128)(2,1)S(1)}, bf16[2,128,1024]{2,1,0:T(8,128)(2,1)S(1)}, u32[]{:S(2)}, u32[]{:S(2)}) collective-permute-start(bf16[2,128,1024]{2,1,0:T(8,128)(2,1)S(1)} %add.152), channel_id=1, source_target_pairs={{16,8},{8,16},{20,12},{12,20},{17,9},{9,17},{21,13},{13,21},{18,10... | collective-permute-start | bytes 1572872 | tf_op jit(solution)/shard_map/ppermute | solution.py:373
  73.4 10.6 %collective-permute-start.16 = (bf16[2,128,1024]{2,1,0:T(8,128)(2,1)S(1)}, bf16[2,128,1024]{2,1,0:T(8,128)(2,1)S(1)}, u32[]{:S(2)}, u32[]{:S(2)}) collective-permute-start(bf16[2,128,1024]{2,1,0:T(8,128)(2,1)S(1)} %add.147), channel_id=1, source_target_pairs={{16,8},{8,16},{20,12},{12,20},{17,9},{9,17},{21,13},{13,21},{18,10... | collective-permute-start | bytes 1572872 | tf_op jit(solution)/shard_map/ppermute | solution.py:373
  81.4 47.5 %collective-permute-start.5 = (bf16[256,3072]{1,0:T(8,128)(2,1)S(1)}, bf16[256,3072]{1,0:T(8,128)(2,1)}, u32[]{:S(2)}, u32[]{:S(2)}) collective-permute-start(bf16[256,3072]{1,0:T(8,128)(2,1)S(1)} %copy-done), channel_id=1, source_target_pairs={{0,1},{1,0},{2,3},{3,2},{4,5},{5,4},{6,7},{7,6},{8,9},{9,8},{10,11... | collective-permute-start | bytes 4718600 | tf_op jit(solution)/shard_map/ppermute | solution.py:347
  81.4 47.6 %collective-permute-start.40 = (bf16[256,3072]{1,0:T(8,128)(2,1)}, bf16[256,3072]{1,0:T(8,128)(2,1)}, u32[]{:S(2)}, u32[]{:S(2)}) collective-permute-start(bf16[256,3072]{1,0:T(8,128)(2,1)} %refs_18_.1), channel_id=1, source_target_pairs={{0,2},{1,3},{2,0},{3,1},{4,6},{5,7},{6,4},{7,5},{8,10},{9,11},{10,... | collective-permute-start | bytes 4718600 | tf_op jit(solution)/shard_map/ppermute | solution.py:347
  82.2 10.7 %collective-permute-start.2 = (bf16[2,128,1024]{2,1,0:T(8,128)(2,1)S(1)}, bf16[2,128,1024]{2,1,0:T(8,128)(2,1)S(1)}, u32[]{:S(2)}, u32[]{:S(2)}) collective-permute-start(bf16[2,128,1024]{2,1,0:T(8,128)(2,1)S(1)} %add.139), channel_id=1, source_target_pairs={{16,8},{8,16},{20,12},{12,20},{17,9},{9,17},{21,13},{13,21},{18,10... | collective-permute-start | bytes 1572872 | tf_op jit(solution)/shard_map/ppermute | solution.py:373
  84.0 27.6 %collective-permute-start.33 = (bf16[2,128,1024]{2,1,0:T(8,128)(2,1)}, bf16[2,128,1024]{2,1,0:T(8,128)(2,1)}, u32[]{:S(2)}, u32[]{:S(2)}) collective-permute-start(bf16[2,128,1024]{2,1,0:T(8,128)(2,1)} %add.159), channel_id=1, source_target_pairs={{8,0},{16,24},{12,4},{20,28},{9,1},{17,25},{13,5},{21,29},{10,2},{... | collective-permute-start | bytes 1572872 | tf_op jit(solution)/shard_map/ppermute | solution.py:373
  91.9 56.6 %collective-permute-start.9 = (bf16[256,3072]{1,0:T(8,128)(2,1)S(1)}, bf16[256,3072]{1,0:T(8,128)(2,1)}, u32[]{:S(2)}, u32[]{:S(2)}) collective-permute-start(bf16[256,3072]{1,0:T(8,128)(2,1)S(1)} %collective-permute-done.7.refs_9_), channel_id=1, source_target_pairs={{0,1},{1,0},{2,3},{3,2},{4,5},{5,4},{6,7},{7,6},{8,9},{9,8},{10,11... | collective-permute-start | bytes 4718600 | tf_op jit(solution)/shard_map/ppermute | solution.py:347
  93.8 32.7 %collective-permute-start.25 = (bf16[2,128,1024]{2,1,0:T(8,128)(2,1)}, bf16[2,128,1024]{2,1,0:T(8,128)(2,1)}, u32[]{:S(2)}, u32[]{:S(2)}) collective-permute-start(bf16[2,128,1024]{2,1,0:T(8,128)(2,1)} %add.154), channel_id=1, source_target_pairs={{8,0},{16,24},{12,4},{20,28},{9,1},{17,25},{13,5},{21,29},{10,2},{... | collective-permute-start | bytes 1572872 | tf_op jit(solution)/shard_map/ppermute | solution.py:373
  96.7 16.2 %copy-start.26 = (bf16[2,128,1024]{2,1,0:T(8,128)(2,1)S(1)}, bf16[2,128,1024]{2,1,0:T(8,128)(2,1)}, u32[]{:S(2)}) copy-start(bf16[2,128,1024]{2,1,0:T(8,128)(2,1)} %copy-done.25) | copy-start | bytes 1572868
  96.7 16.2 %copy-start.34 = (bf16[2,128,1024]{2,1,0:T(8,128)(2,1)S(1)}, bf16[2,128,1024]{2,1,0:T(8,128)(2,1)}, u32[]{:S(2)}) copy-start(bf16[2,128,1024]{2,1,0:T(8,128)(2,1)} %copy-done.33) | copy-start | bytes 1572868
  98.2 29.6 %copy-start.28 = (bf16[2,128,1024]{2,1,0:T(8,128)(2,1)S(1)}, bf16[2,128,1024]{2,1,0:T(8,128)(2,1)}, u32[]{:S(2)}) copy-start(bf16[2,128,1024]{2,1,0:T(8,128)(2,1)} %copy-done.27) | copy-start | bytes 1572868
  98.2 29.6 %copy-start.32 = (bf16[2,128,1024]{2,1,0:T(8,128)(2,1)S(1)}, bf16[2,128,1024]{2,1,0:T(8,128)(2,1)}, u32[]{:S(2)}) copy-start(bf16[2,128,1024]{2,1,0:T(8,128)(2,1)} %copy-done.31) | copy-start | bytes 1572868
  98.4 40.7 %copy-start.20 = (bf16[2,128,1024]{2,1,0:T(8,128)(2,1)S(1)}, bf16[2,128,1024]{2,1,0:T(8,128)(2,1)}, u32[]{:S(2)}) copy-start(bf16[2,128,1024]{2,1,0:T(8,128)(2,1)} %copy-done.19) | copy-start | bytes 1572868
  98.4 40.7 %copy-start.22 = (bf16[2,128,1024]{2,1,0:T(8,128)(2,1)S(1)}, bf16[2,128,1024]{2,1,0:T(8,128)(2,1)}, u32[]{:S(2)}) copy-start(bf16[2,128,1024]{2,1,0:T(8,128)(2,1)} %copy-done.21) | copy-start | bytes 1572868
  111.6 26.0 %collective-permute-start.17 = (bf16[2,128,1024]{2,1,0:T(8,128)(2,1)S(1)}, bf16[2,128,1024]{2,1,0:T(8,128)(2,1)S(1)}, u32[]{:S(2)}, u32[]{:S(2)}) collective-permute-start(bf16[2,128,1024]{2,1,0:T(8,128)(2,1)S(1)} %add.149), channel_id=1, source_target_pairs={{8,0},{16,24},{12,4},{20,28},{9,1},{17,25},{13,5},{21,29},{10,2},{... | collective-permute-start | bytes 1572872 | tf_op jit(solution)/shard_map/ppermute | solution.py:373
  126.5 19.1 %collective-permute-start.3 = (bf16[2,128,1024]{2,1,0:T(8,128)(2,1)S(1)}, bf16[2,128,1024]{2,1,0:T(8,128)(2,1)S(1)}, u32[]{:S(2)}, u32[]{:S(2)}) collective-permute-start(bf16[2,128,1024]{2,1,0:T(8,128)(2,1)S(1)} %add.141), channel_id=1, source_target_pairs={{8,0},{16,24},{12,4},{20,28},{9,1},{17,25},{13,5},{21,29},{10,2},{... | collective-permute-start | bytes 1572872 | tf_op jit(solution)/shard_map/ppermute | solution.py:373
  128.9 18.2 %copy-start.24 = (bf16[2,128,1024]{2,1,0:T(8,128)(2,1)S(1)}, bf16[2,128,1024]{2,1,0:T(8,128)(2,1)}, u32[]{:S(2)}) copy-start(bf16[2,128,1024]{2,1,0:T(8,128)(2,1)} %copy-done.23) | copy-start | bytes 1572868
  129.0 52.2 %collective-permute-start.38 = (bf16[256,3072]{1,0:T(8,128)(2,1)}, bf16[256,3072]{1,0:T(8,128)(2,1)S(1)}, u32[]{:S(2)}, u32[]{:S(2)}) collective-permute-start(bf16[256,3072]{1,0:T(8,128)(2,1)} %refs_18_.1), channel_id=1, source_target_pairs={{0,1},{1,0},{2,3},{3,2},{4,5},{5,4},{6,7},{7,6},{8,9},{9,8},{10,11... | collective-permute-start | bytes 4718600 | tf_op jit(solution)/shard_map/ppermute | solution.py:347
  129.1 53.9 %collective-permute-start.42 = (bf16[256,3072]{1,0:T(8,128)(2,1)}, bf16[256,3072]{1,0:T(8,128)(2,1)S(1)}, u32[]{:S(2)}, u32[]{:S(2)}) collective-permute-start(bf16[256,3072]{1,0:T(8,128)(2,1)} %collective-permute-done.40.refs_22_), channel_id=1, source_target_pairs={{0,1},{1,0},{2,3},{3,2},{4,5},{5,4},{6,7},{7,6},{8,9},{9,8},{10,11... | collective-permute-start | bytes 4718600 | tf_op jit(solution)/shard_map/ppermute | solution.py:347
  137.6 10.9 %collective-permute-start.34 = (bf16[2,128,1024]{2,1,0:T(8,128)(2,1)S(1)}, bf16[2,128,1024]{2,1,0:T(8,128)(2,1)S(1)}, u32[]{:S(2)}, u32[]{:S(2)}) collective-permute-start(bf16[2,128,1024]{2,1,0:T(8,128)(2,1)S(1)} %add_add_fusion.refs_1_), channel_id=1, source_target_pairs={{0,4},{4,0},{8,12},{12,8},{16,20},{20,16},{24,28},{28,24},{1,5},{5... | collective-permute-start | bytes 1572872 | tf_op jit(solution)/shard_map/ppermute | solution.py:377
  139.1 10.9 %copy-start.14 = (bf16[256,1024]{1,0:T(8,128)(2,1)S(1)}, bf16[256,1024]{1,0:T(8,128)(2,1)}, u32[]{:S(2)}) copy-start(bf16[256,1024]{1,0:T(8,128)(2,1)} %copy-done.13) | copy-start | bytes 1572868
  145.6 14.8 %collective-permute-start.26 = (bf16[2,128,1024]{2,1,0:T(8,128)(2,1)S(1)}, bf16[2,128,1024]{2,1,0:T(8,128)(2,1)S(1)}, u32[]{:S(2)}, u32[]{:S(2)}) collective-permute-start(bf16[2,128,1024]{2,1,0:T(8,128)(2,1)S(1)} %add_add_fusion.1.refs_1_), channel_id=1, source_target_pairs={{0,4},{4,0},{8,12},{12,8},{16,20},{20,16},{24,28},{28,24},{1,5},{5... | collective-permute-start | bytes 1572872 | tf_op jit(solution)/shard_map/ppermute | solution.py:377
  148.5 22.3 %collective-permute-start.43 = (bf16[256,1024]{1,0:T(8,128)(2,1)S(1)}, bf16[256,1024]{1,0:T(8,128)(2,1)S(1)}, u32[]{:S(2)}, u32[]{:S(2)}) collective-permute-start(bf16[256,1024]{1,0:T(8,128)(2,1)S(1)} %copy-done.6), channel_id=1, source_target_pairs={{0,1},{1,0},{2,3},{3,2},{4,5},{5,4},{6,7},{7,6},{8,9},{9,8},{10,11... | collective-permute-start | bytes 1572872 | tf_op jit(solution)/shard_map/ppermute | solution.py:347
  148.5 23.2 %collective-permute-start.18 = (bf16[2,128,1024]{2,1,0:T(8,128)(2,1)S(1)}, bf16[2,128,1024]{2,1,0:T(8,128)(2,1)S(1)}, u32[]{:S(2)}, u32[]{:S(2)}) collective-permute-start(bf16[2,128,1024]{2,1,0:T(8,128)(2,1)S(1)} %add_add_fusion.2.refs_1_), channel_id=1, source_target_pairs={{0,4},{4,0},{8,12},{12,8},{16,20},{20,16},{24,28},{28,24},{1,5},{5... | collective-permute-start | bytes 1572872 | tf_op jit(solution)/shard_map/ppermute | solution.py:377
  160.4 21.4 %collective-permute-start.4 = (bf16[2,128,1024]{2,1,0:T(8,128)(2,1)S(1)}, bf16[2,128,1024]{2,1,0:T(8,128)(2,1)S(1)}, u32[]{:S(2)}, u32[]{:S(2)}) collective-permute-start(bf16[2,128,1024]{2,1,0:T(8,128)(2,1)S(1)} %add_add_fusion.3.refs_1_), channel_id=1, source_target_pairs={{0,4},{4,0},{8,12},{12,8},{16,20},{20,16},{24,28},{28,24},{1,5},{5... | collective-permute-start | bytes 1572872 | tf_op jit(solution)/shard_map/ppermute | solution.py:377
  170.8 12.7 %collective-permute-start.35 = (bf16[4,32,1024]{2,1,0:T(8,128)(2,1)S(1)}, bf16[4,32,1024]{2,1,0:T(8,128)(2,1)S(1)}, u32[]{:S(2)}, u32[]{:S(2)}) collective-permute-start(bf16[4,32,1024]{2,1,0:T(8,128)(2,1)S(1)} %get-tuple-element.52), channel_id=1, source_target_pairs={{0,1},{1,0},{2,3},{3,2},{4,5},{5,4},{6,7},{7,6},{8,9},{9,8},{10,11... | collective-permute-start | bytes 786440 | tf_op jit(solution)/shard_map/ppermute | solution.py:347
  171.7 12.7 %collective-permute-start.36 = (bf16[4,32,1024]{2,1,0:T(8,128)(2,1)S(1)}, bf16[4,32,1024]{2,1,0:T(8,128)(2,1)S(1)}, u32[]{:S(2)}, u32[]{:S(2)}) collective-permute-start(bf16[4,32,1024]{2,1,0:T(8,128)(2,1)S(1)} %get-tuple-element.53), channel_id=1, source_target_pairs={{0,2},{1,3},{2,0},{3,1},{4,6},{5,7},{6,4},{7,5},{8,10},{9,11},{10,... | collective-permute-start | bytes 786440 | tf_op jit(solution)/shard_map/ppermute | solution.py:347
  181.2 12.8 %collective-permute-start.37 = (bf16[4,32,1024]{2,1,0:T(8,128)(2,1)S(1)}, bf16[4,32,1024]{2,1,0:T(8,128)(2,1)S(1)}, u32[]{:S(2)}, u32[]{:S(2)}) collective-permute-start(bf16[4,32,1024]{2,1,0:T(8,128)(2,1)S(1)} %get-tuple-element.54), channel_id=1, source_target_pairs={{0,3},{1,2},{2,1},{3,0},{4,7},{5,6},{6,5},{7,4},{8,11},{9,10},{10,... | collective-permute-start | bytes 786440 | tf_op jit(solution)/shard_map/ppermute | solution.py:347
  181.8 12.8 %collective-permute-start.27 = (bf16[4,32,1024]{2,1,0:T(8,128)(2,1)S(1)}, bf16[4,32,1024]{2,1,0:T(8,128)(2,1)S(1)}, u32[]{:S(2)}, u32[]{:S(2)}) collective-permute-start(bf16[4,32,1024]{2,1,0:T(8,128)(2,1)S(1)} %get-tuple-element.46), channel_id=1, source_target_pairs={{0,1},{1,0},{2,3},{3,2},{4,5},{5,4},{6,7},{7,6},{8,9},{9,8},{10,11... | collective-permute-start | bytes 786440 | tf_op jit(solution)/shard_map/ppermute | solution.py:347
  182.9 11.1 %copy-start.36 = (bf16[256,3072]{1,0:T(8,128)(2,1)}, bf16[256,3072]{1,0:T(8,128)(2,1)S(1)}, u32[]{:S(2)}) copy-start(bf16[256,3072]{1,0:T(8,128)(2,1)S(1)} %collective-permute-done.42.refs_24_) | copy-start | bytes 4718596
  182.9 12.7 %collective-permute-start.28 = (bf16[4,32,1024]{2,1,0:T(8,128)(2,1)S(1)}, bf16[4,32,1024]{2,1,0:T(8,128)(2,1)S(1)}, u32[]{:S(2)}, u32[]{:S(2)}) collective-permute-start(bf16[4,32,1024]{2,1,0:T(8,128)(2,1)S(1)} %get-tuple-element.47), channel_id=1, source_target_pairs={{0,2},{1,3},{2,0},{3,1},{4,6},{5,7},{6,4},{7,5},{8,10},{9,11},{10,... | collective-permute-start | bytes 786440 | tf_op jit(solution)/shard_map/ppermute | solution.py:347
  183.4 17.6 %collective-permute-start.29 = (bf16[4,32,1024]{2,1,0:T(8,128)(2,1)S(1)}, bf16[4,32,1024]{2,1,0:T(8,128)(2,1)S(1)}, u32[]{:S(2)}, u32[]{:S(2)}) collective-permute-start(bf16[4,32,1024]{2,1,0:T(8,128)(2,1)S(1)} %get-tuple-element.48), channel_id=1, source_target_pairs={{0,3},{1,2},{2,1},{3,0},{4,7},{5,6},{6,5},{7,4},{8,11},{9,10},{10,... | collective-permute-start | bytes 786440 | tf_op jit(solution)/shard_map/ppermute | solution.py:347
  184.4 39.1 %copy-start.4 = (bf16[256,1024]{1,0:T(8,128)(2,1)S(1)}, bf16[256,1024]{1,0:T(8,128)(2,1)}, u32[]{:S(2)}) copy-start(bf16[256,1024]{1,0:T(8,128)(2,1)} %refs_19_.1) | copy-start | bytes 1572868
  184.4 39.1 %copy-start.8 = (bf16[256,1024]{1,0:T(8,128)(2,1)S(1)}, bf16[256,1024]{1,0:T(8,128)(2,1)}, u32[]{:S(2)}) copy-start(bf16[256,1024]{1,0:T(8,128)(2,1)} %copy-done.7) | copy-start | bytes 1572868
  184.4 39.1 %copy-start.15 = (f32[1024]{0:T(1024)S(1)}, f32[1024]{0:T(1024)}, u32[]{:S(2)}) copy-start(f32[1024]{0:T(1024)} %param.17) | copy-start | bytes 12292
  184.4 18.3 %collective-permute-start.19 = (bf16[4,32,1024]{2,1,0:T(8,128)(2,1)S(1)}, bf16[4,32,1024]{2,1,0:T(8,128)(2,1)S(1)}, u32[]{:S(2)}, u32[]{:S(2)}) collective-permute-start(bf16[4,32,1024]{2,1,0:T(8,128)(2,1)S(1)} %get-tuple-element.40), channel_id=1, source_target_pairs={{0,1},{1,0},{2,3},{3,2},{4,5},{5,4},{6,7},{7,6},{8,9},{9,8},{10,11... | collective-permute-start | bytes 786440 | tf_op jit(solution)/shard_map/ppermute | solution.py:347
  194.0 12.8 %collective-permute-start.20 = (bf16[4,32,1024]{2,1,0:T(8,128)(2,1)S(1)}, bf16[4,32,1024]{2,1,0:T(8,128)(2,1)S(1)}, u32[]{:S(2)}, u32[]{:S(2)}) collective-permute-start(bf16[4,32,1024]{2,1,0:T(8,128)(2,1)S(1)} %get-tuple-element.41), channel_id=1, source_target_pairs={{0,2},{1,3},{2,0},{3,1},{4,6},{5,7},{6,4},{7,5},{8,10},{9,11},{10,... | collective-permute-start | bytes 786440 | tf_op jit(solution)/shard_map/ppermute | solution.py:347
  194.6 17.7 %collective-permute-start.21 = (bf16[4,32,1024]{2,1,0:T(8,128)(2,1)S(1)}, bf16[4,32,1024]{2,1,0:T(8,128)(2,1)S(1)}, u32[]{:S(2)}, u32[]{:S(2)}) collective-permute-start(bf16[4,32,1024]{2,1,0:T(8,128)(2,1)S(1)} %get-tuple-element.42), channel_id=1, source_target_pairs={{0,3},{1,2},{2,1},{3,0},{4,7},{5,6},{6,5},{7,4},{8,11},{9,10},{10,... | collective-permute-start | bytes 786440 | tf_op jit(solution)/shard_map/ppermute | solution.py:347
  195.6 16.7 %collective-permute-start.11 = (bf16[4,32,1024]{2,1,0:T(8,128)(2,1)S(1)}, bf16[4,32,1024]{2,1,0:T(8,128)(2,1)S(1)}, u32[]{:S(2)}, u32[]{:S(2)}) collective-permute-start(bf16[4,32,1024]{2,1,0:T(8,128)(2,1)S(1)} %get-tuple-element.34), channel_id=1, source_target_pairs={{0,1},{1,0},{2,3},{3,2},{4,5},{5,4},{6,7},{7,6},{8,9},{9,8},{10,11... | collective-permute-start | bytes 786440 | tf_op jit(solution)/shard_map/ppermute | solution.py:347
  201.1 17.0 %collective-permute-start.12 = (bf16[4,32,1024]{2,1,0:T(8,128)(2,1)S(1)}, bf16[4,32,1024]{2,1,0:T(8,128)(2,1)S(1)}, u32[]{:S(2)}, u32[]{:S(2)}) collective-permute-start(bf16[4,32,1024]{2,1,0:T(8,128)(2,1)S(1)} %get-tuple-element.35), channel_id=1, source_target_pairs={{0,2},{1,3},{2,0},{3,1},{4,6},{5,7},{6,4},{7,5},{8,10},{9,11},{10,... | collective-permute-start | bytes 786440 | tf_op jit(solution)/shard_map/ppermute | solution.py:347
  202.7 20.9 %collective-permute-start.13 = (bf16[4,32,1024]{2,1,0:T(8,128)(2,1)S(1)}, bf16[4,32,1024]{2,1,0:T(8,128)(2,1)S(1)}, u32[]{:S(2)}, u32[]{:S(2)}) collective-permute-start(bf16[4,32,1024]{2,1,0:T(8,128)(2,1)S(1)} %get-tuple-element.36), channel_id=1, source_target_pairs={{0,3},{1,2},{2,1},{3,0},{4,7},{5,6},{6,5},{7,4},{8,11},{9,10},{10,... | collective-permute-start | bytes 786440 | tf_op jit(solution)/shard_map/ppermute | solution.py:347
  (18 other events, 126.1 us)
